TPU v7x, 256 devices: a whole 4x4x8 slice. The times are simulated.
256 devices in a mesh: grp: 16 (over z_lo, y), dev: 16 (over x, z_hi, core).
Axes of the slice: x: 4, y: 4, z: 8 (z_hi: 2, z_lo: 4; z = z_hi * 4 + z_lo), core: 2. Of those that a mesh axis runs over, the one named last changes fastest.
Arguments:
- right_side: float32 [16, 16, 3, 4096], P('grp', 'dev'), may hold values from -15 to 15
- elem_nodes: int32 [16, 16, 27, 512], P('grp', 'dev'), may hold values from 0 to 4095, as said below
- elem_coef: float32 [16, 16, 512], P('grp', 'dev'), may hold values from 0.2 to 5
- node_mass: float32 [16, 16, 3, 4096], P('grp', 'dev'), may hold values from 0.5 to 4
- face_slots: int32 [16, 16, 4, 512], P('grp', 'dev'), may hold values from 0 to 4096, as said below
- coarse_nodes: int32 [16, 16, 4, 4096], P('grp', 'dev'), may hold values from 0 to 1535, as said below
- coarse_weights: float32 [16, 16, 4, 4096], P('grp', 'dev'), may hold values from 0.1 to 0.6
- elem_matrix: float32 [81, 81], replicated, may hold values from -1 to 2, as said below
- chol_inverse: float32 [4608, 4608], P('dev'), may hold values from -1 to 1, as said below
Outputs:
- preconditioned: float32 [16, 16, 3, 4096], P('grp', 'dev')
Inputs may be any that keep to these rules, and one draw needn't show every extreme that they name: `elem_nodes`: the 27 entries of one element are distinct. `face_slots`: an entry 4096 is padding; the other entries of one subdomain are distinct. Slot p of a face and slot p of the neighbour's face back name the same shared node: both are padding or neither. Live slots come first in a face; faces with no neighbour subdomain are all padding; some face has all 512 slots live. `coarse_nodes`: the entries of subdomain (g, d) lie in the 64 coarse nodes from ((16 * g + d) * 1536) // 256 on, counted modulo 1536. `elem_matrix`: Symmetric; each diagonal entry is positive and exceeds the sum of the magnitudes of the other entries of its row. `chol_inverse`: lower triangular with a positive diagonal.
All inputs are finite; a program needn't handle non-finite values.
Results may differ from a plain program's by a relative error of at most 0.0001.
Values sent between devices are 32-bit elements; how exact they have to be, the bound alone decides.
A program may use at most 128 MiB of HBM per device.

v0:
```python
import jax
import jax.numpy as jnp
from jax import lax
from jax.sharding import PartitionSpec as P

POST = 2


DAMPING = 0.6
PRECISE = lax.Precision.HIGHEST


def with_halo(value, sides, width):
    edges = {}
    for axis, dim in sides:
        size, length = (lax.axis_size(axis), value.shape[dim])
        up = [(i, (i + 1) % size) for i in range(size - 1)]
        last = lax.slice_in_dim(value, length - width, length, axis=dim)
        initial = lax.slice_in_dim(value, 0, width, axis=dim)
        edges[dim] = (
            lax.ppermute(last, axis, up),
            lax.ppermute(initial, axis, [(b, a) for a, b in up]),
        )
    done = []
    for _, dim in sides:
        low, high = edges[dim]
        around = [(width, width) if d in done else (0, 0) for d in range(value.ndim)]
        value = jnp.concatenate([jnp.pad(low, around), value, jnp.pad(high, around)], axis=dim)
        done.append(dim)
    return value


def in_blocks(value, dim, length):
    before, after = (value.shape[:dim], value.shape[dim + 1 :])
    return jnp.moveaxis(value.reshape(*before, length, -1, *after), dim, 0)


def sum_at_owner(value, axis, dim):
    length = lax.axis_size(axis)
    tiles = lax.all_to_all(in_blocks(value, dim, length), axis, 0, 0, tiled=True)
    return jnp.sum(tiles, axis=0)


def from_everyone(value, axis):
    length = lax.axis_size(axis)
    return lax.all_to_all(
        jnp.broadcast_to(value[None], (length, *value.shape)), axis, 0, 0, tiled=True
    )


def of_everyone(value, axis):
    everything = from_everyone(value, axis)
    return jnp.sum(everything, axis=0)


def in_order(tiles, dim):
    lengths = list(tiles.shape[1:])
    lengths[dim] *= tiles.shape[0]
    return jnp.moveaxis(tiles, 0, dim).reshape(lengths)


def collect(value, axis, dim):
    return in_order(from_everyone(value, axis), dim)


def element_apply(matrix, field, node_index, elem_scale, mass_here):
    elem_count = node_index.shape[1]
    gathered = field[:, node_index].reshape(81, elem_count)
    product = jnp.dot(matrix, gathered, precision=PRECISE) * elem_scale[None, :]
    summed = jnp.zeros_like(field).at[:, node_index].add(product.reshape(3, 27, elem_count))
    return summed + mass_here * field


def exchange_faces(field, face_index):
    outgoing = field.at[:, face_index].get(mode="fill", fill_value=0.0)
    padded = with_halo(outgoing[None, None], (("grp", 0), ("dev", 1)), 1)
    received = jnp.stack(
        [padded[0, 1, :, 1], padded[2, 1, :, 0], padded[1, 0, :, 3], padded[1, 2, :, 2]], axis=1
    )
    return field.at[:, face_index].add(received, mode="drop")


def restrict(coarse_width, field, coarse_index, weights):
    values = weights[None] * field[:, None, :]
    return (
        jnp.zeros((3, coarse_width), field.dtype)
        .at[:, coarse_index]
        .add(values)
        .reshape(3 * coarse_width)
    )


def prolong(coarse, coarse_index, weights):
    coarse_table = coarse.reshape(3, coarse.shape[0] // 3)
    return jnp.sum(weights[None] * coarse_table[:, coarse_index], axis=1)


def local(
    right_side,
    elem_nodes,
    elem_coef,
    node_mass,
    face_slots,
    coarse_nodes,
    coarse_weights,
    elem_matrix,
    chol_inverse,
):
    target = right_side[0, 0]
    node_index = elem_nodes[0, 0]
    elem_scale = elem_coef[0, 0]
    mass_here = node_mass[0, 0]
    face_index = face_slots[0, 0]
    coarse_index = coarse_nodes[0, 0]
    weights = coarse_weights[0, 0]
    coarse_width = chol_inverse.shape[1] // 3

    def operate(field):
        return exchange_faces(
            element_apply(elem_matrix, field, node_index, elem_scale, mass_here), face_index
        )

    main_diag = jnp.diagonal(elem_matrix).reshape(3, 27)
    local_diag = (
        jnp.zeros_like(mass_here)
        .at[:, node_index]
        .add(main_diag[:, :, None] * elem_scale[None, None, :])
        + mass_here
    )
    diag_total = exchange_faces(local_diag, face_index)
    iterate = DAMPING * target / diag_total
    iterate = iterate + DAMPING * (target - operate(iterate)) / diag_total
    residual = target - operate(iterate)
    local_sum = restrict(coarse_width, residual, coarse_index, weights)
    slice_sum = sum_at_owner(local_sum, "dev", 0)
    slice_sum = of_everyone(slice_sum, "grp")
    halfway = jnp.dot(chol_inverse, collect(slice_sum, "dev", 0), precision=PRECISE)
    partial_terms = jnp.dot(halfway, chol_inverse, precision=PRECISE)
    correction = of_everyone(partial_terms, "dev")
    iterate = iterate + prolong(correction, coarse_index, weights)
    for sweep_index in range(POST):
        iterate = iterate + DAMPING * (target - operate(iterate)) / diag_total
    return iterate[None, None]


def solution(mesh):
    return jax.shard_map(
        local,
        mesh=mesh,
        in_specs=(
            P("grp", "dev", None, None),
            P("grp", "dev", None, None),
            P("grp", "dev", None),
            P("grp", "dev", None, None),
            P("grp", "dev", None, None),
            P("grp", "dev", None, None),
            P("grp", "dev", None, None),
            P(),
            P("dev", None),
        ),
        out_specs=P("grp", "dev", None, None),
        check_vma=False,
    )
```

profile of v0, /device:TPU:1, one launch (start us, length us, event | category | flops | bytes accessed | tf_op | source)
XLA Modules:
  0.0 983.4 jit_solution(12503001600006664610)
XLA Ops:
  11.6 74.9 %scatter_fusion = f32[3,4096]{0,1:T(8,128)S(1)} fusion(f32[3,4096]{0,1:T(8,128)S(1)} %copy-done.3, s32[13824]{0:T(1024)S(1)} %reshape.279, f32[13824,3]{1,0:T(8,128)} %bitcast.202), kind=kCustom, calls=%fused_computation.11 | custom fusion | flops 41472 | bytes 552960 | tf_op jit(solution)/shard_map/scatter-add | solution.py:127
  86.4 7.6 gather_fusion.1
  115.3 13.6 %scatter_fusion.1 = f32[3,4096]{0,1:T(8,128)} fusion(f32[3,4096]{0,1:T(8,128)} %copy-done.4, s32[2048]{0:T(1024)S(1)} %bitcast.222, f32[2048,3]{1,0:T(8,128)} %bitcast.204), kind=kCustom, calls=%fused_computation.12 | custom fusion | flops 6144 | bytes 81920 | tf_op jit(solution)/shard_map/scatter-add | solution.py:80
  133.7 27.7 %gather_fusion.2 = f32[13824,3]{1,0:T(8,128)} fusion(f32[3,4096]{0,1:T(8,128)} %get-tuple-element.11, s32[14336]{0:T(1024)S(1)} %pad_clamp_fusion), kind=kCustom, calls=%fused_computation.2 | custom fusion | bytes 387072 | tf_op jit(solution)/shard_map/gather | solution.py:68
  170.9 69.5 %scatter_fusion.2 = f32[3,4096]{0,1:T(8,128)} fusion(f32[3,4096]{0,1:T(8,128)} %get-tuple-element.12, s32[13824]{0:T(1024)S(1)} %reshape.279, f32[13824,3]{1,0:T(8,128)} %bitcast.195), kind=kCustom, calls=%fused_computation.13 | custom fusion | flops 41472 | bytes 552960 | tf_op jit(solution)/shard_map/scatter-add | solution.py:70
  240.4 9.2 gather_fusion.3
  268.5 13.6 %scatter_fusion.3 = f32[3,4096]{0,1:T(8,128)} fusion(f32[3,4096]{0,1:T(8,128)} %scatter_fusion.2, s32[2048]{0:T(1024)S(1)} %bitcast.223, f32[2048,3]{1,0:T(8,128)} %bitcast.205), kind=kCustom, calls=%fused_computation.14 | custom fusion | flops 6144 | bytes 81920 | tf_op jit(solution)/shard_map/scatter-add | solution.py:80
  287.8 27.7 %gather_fusion.4 = f32[13824,3]{1,0:T(8,128)} fusion(f32[3,4096]{0,1:T(8,128)} %get-tuple-element.10, s32[14336]{0:T(1024)S(1)} %pad_clamp_fusion), kind=kCustom, calls=%fused_computation.4 | custom fusion | bytes 387072 | tf_op jit(solution)/shard_map/gather | solution.py:68
  325.0 69.6 %scatter_fusion.4 = f32[3,4096]{0,1:T(8,128)} fusion(f32[3,4096]{0,1:T(8,128)} %get-tuple-element.9, s32[13824]{0:T(1024)S(1)} %reshape.279, f32[13824,3]{1,0:T(8,128)} %bitcast.196), kind=kCustom, calls=%fused_computation.15 | custom fusion | flops 41472 | bytes 552960 | tf_op jit(solution)/shard_map/scatter-add | solution.py:70
  394.6 9.1 gather_fusion.5
  422.7 13.7 %scatter_fusion.5 = f32[3,4096]{0,1:T(8,128)} fusion(f32[3,4096]{0,1:T(8,128)} %scatter_fusion.4, s32[2048]{0:T(1024)S(1)} %bitcast.224, f32[2048,3]{1,0:T(8,128)} %bitcast.206), kind=kCustom, calls=%fused_computation.16 | custom fusion | flops 6144 | bytes 81920 | tf_op jit(solution)/shard_map/scatter-add | solution.py:80
  443.5 87.8 %scatter_custom_fusion.6 = f32[3,1536]{0,1:T(8,128)S(1)} fusion(s32[16384]{0:T(1024)S(1)} %bitcast.229, f32[16384,3]{1,0:T(8,128)} %bitcast.193, f32[]{:T(128)} %constant.10.clone.1), kind=kCustom, calls=%fused_computation.52 | custom fusion | flops 49152 | bytes 18944 | tf_op jit(solution)/shard_map/scatter-add | solution.py:88
  531.7 22.7 %all_to_all.28 = f32[16,1,288]{2,1,0:T(1,128)S(1)} all-to-all(f32[16,1,288]{2,1,0:T(1,128)S(1)} %all_to_all.23), channel_id=1, replica_groups=mesh['grp'=16,'dev'=16] {'dev'}, dimensions={0} | all-to-all | bytes 36864 | tf_op jit(solution)/shard_map/all_to_all | solution.py:40
  554.5 18.1 %all_to_all.29 = f32[16,1,288]{2,1,0:T(1,128)S(1)} all-to-all(f32[16,1,288]{2,1,0:T(1,128)S(1)} %broadcast_in_dim.18), channel_id=1, replica_groups=mesh['grp'=16,'dev'=16] {'grp'}, dimensions={0} | all-to-all | bytes 36864 | tf_op jit(solution)/shard_map/all_to_all | solution.py:46
  572.7 14.0 %all_to_all.30 = f32[16,1,288]{2,1,0:T(1,128)S(1)} all-to-all(f32[16,1,288]{2,1,0:T(1,128)S(1)} %broadcast_in_dim.19), channel_id=1, replica_groups=mesh['grp'=16,'dev'=16] {'dev'}, dimensions={0} | all-to-all | bytes 36864 | tf_op jit(solution)/shard_map/all_to_all | solution.py:46
  602.8 11.5 %all-to-all-done.3 = f32[16,1,4608]{2,1,0:T(1,128)S(1)} async-done(((f32[16,1,4608]{2,1,0:T(1,128)}), f32[16,1,4608]{2,1,0:T(1,128)S(1)}, u32[]{:S(2)}, u32[]{:S(2)}) %all-to-all-start.3) | async-done | bytes 294944 | tf_op jit(solution)/shard_map/all_to_all | solution.py:46
  614.8 54.4 %gather_fusion.6 = f32[16384,3]{1,0:T(8,128)} fusion(f32[3,1536]{0,1:T(8,128)S(1)} %copy.99, s32[16384]{0:T(1024)S(1)} %broadcast_clamp_fusion), kind=kCustom, calls=%fused_computation.6 | custom fusion | bytes 458752 | tf_op jit(solution)/shard_map/gather | solution.py:95
  677.0 27.7 %gather_fusion.7 = f32[13824,3]{1,0:T(8,128)} fusion(f32[3,4096]{0,1:T(8,128)} %get-tuple-element.8, s32[14336]{0:T(1024)S(1)} %pad_clamp_fusion), kind=kCustom, calls=%fused_computation.7 | custom fusion | bytes 387072 | tf_op jit(solution)/shard_map/gather | solution.py:68
  714.2 69.5 %scatter_fusion.6 = f32[3,4096]{0,1:T(8,128)} fusion(f32[3,4096]{0,1:T(8,128)} %get-tuple-element.7, s32[13824]{0:T(1024)S(1)} %reshape.279, f32[13824,3]{1,0:T(8,128)} %bitcast.197), kind=kCustom, calls=%fused_computation.18 | custom fusion | flops 41472 | bytes 552960 | tf_op jit(solution)/shard_map/scatter-add | solution.py:70
  783.7 9.2 gather_fusion.8
  811.7 13.6 %scatter_fusion.7 = f32[3,4096]{0,1:T(8,128)} fusion(f32[3,4096]{0,1:T(8,128)} %scatter_fusion.6, s32[2048]{0:T(1024)S(1)} %bitcast.225, f32[2048,3]{1,0:T(8,128)} %bitcast.207), kind=kCustom, calls=%fused_computation.19 | custom fusion | flops 6144 | bytes 81920 | tf_op jit(solution)/shard_map/scatter-add | solution.py:80
  831.4 27.7 %gather_fusion.9 = f32[13824,3]{1,0:T(8,128)} fusion(f32[3,4096]{0,1:T(8,128)} %get-tuple-element.6, s32[14336]{0:T(1024)S(1)} %pad_clamp_fusion), kind=kCustom, calls=%fused_computation.9 | custom fusion | bytes 387072 | tf_op jit(solution)/shard_map/gather | solution.py:68
  868.7 69.6 %scatter_fusion.8 = f32[3,4096]{0,1:T(8,128)} fusion(f32[3,4096]{0,1:T(8,128)} %get-tuple-element.5, s32[13824]{0:T(1024)S(1)} %reshape.279, f32[13824,3]{1,0:T(8,128)} %bitcast.194), kind=kCustom, calls=%fused_computation.20 | custom fusion | flops 41472 | bytes 552960 | tf_op jit(solution)/shard_map/scatter-add | solution.py:70
  962.1 13.3 %scatter_fusion.9 = f32[3,4096]{0,1:T(8,128)} fusion(f32[3,4096]{0,1:T(8,128)} %scatter_fusion.8, s32[2048]{0:T(1024)S(1)} %bitcast.226, f32[2048,3]{1,0:T(8,128)S(1)} %bitcast.203), kind=kCustom, calls=%fused_computation.21 | custom fusion | flops 6144 | bytes 81920 | tf_op jit(solution)/shard_map/scatter-add | solution.py:80
  (163 shorter events, 207.2 us)
Async XLA Ops:
  11.5 101.5 %copy-start.9 = (f32[1,1,3,4096]{3,1,2,0:T(1,128)S(1)}, f32[1,1,3,4096]{3,1,2,0:T(1,128)}, u32[]{:S(2)}) copy-start(f32[1,1,3,4096]{3,1,2,0:T(1,128)} %param.9) | copy-start | bytes 147460
  86.4 26.6 %copy-start.4 = (f32[3,4096]{0,1:T(8,128)}, f32[3,4096]{0,1:T(8,128)S(1)}, u32[]{:S(2)}) copy-start(f32[3,4096]{0,1:T(8,128)S(1)} %scatter_fusion) | copy-start | bytes 147460
  95.6 18.1 %collective-permute-start.3 = (f32[1,1,3,4,512]{4,3,2,1,0:T(4,128)S(1)}, f32[1,1,3,4,512]{4,3,2,1,0:T(4,128)S(1)}, u32[]{:S(2)}, u32[]{:S(2)}) collective-permute-start(f32[1,1,3,4,512]{4,3,2,1,0:T(4,128)S(1)} %bitcast_select_fusion.4), channel_id=1, source_target_pairs={{1,0},{2,1},{3,2},{4,3},{5,4},{6,5},{7,6},{8,7},{9,8},{10,9},{11,1... | collective-permute-start | bytes 73736 | tf_op jit(solution)/shard_map/ppermute | solution.py:22
  100.7 13.0 %collective-permute-start.2 = (f32[1,1,3,4,512]{4,3,2,1,0:T(4,128)S(1)}, f32[1,1,3,4,512]{4,3,2,1,0:T(4,128)S(1)}, u32[]{:S(2)}, u32[]{:S(2)}) collective-permute-start(f32[1,1,3,4,512]{4,3,2,1,0:T(4,128)S(1)} %bitcast_select_fusion.4), channel_id=1, source_target_pairs={{0,1},{1,2},{2,3},{3,4},{4,5},{5,6},{6,7},{7,8},{8,9},{9,10},{10,1... | collective-permute-start | bytes 73736 | tf_op jit(solution)/shard_map/ppermute | solution.py:21
  107.7 6.0 collective-permute-start.1
  109.0 4.9 collective-permute-start
  251.1 15.2 %collective-permute-start.7 = (f32[1,1,3,4,512]{4,3,2,1,0:T(4,128)S(1)}, f32[1,1,3,4,512]{4,3,2,1,0:T(4,128)S(1)}, u32[]{:S(2)}, u32[]{:S(2)}) collective-permute-start(f32[1,1,3,4,512]{4,3,2,1,0:T(4,128)S(1)} %bitcast_select_fusion.3), channel_id=1, source_target_pairs={{1,0},{2,1},{3,2},{4,3},{5,4},{6,5},{7,6},{8,7},{9,8},{10,9},{11,1... | collective-permute-start | bytes 73736 | tf_op jit(solution)/shard_map/ppermute | solution.py:22
  253.1 13.3 %collective-permute-start.6 = (f32[1,1,3,4,512]{4,3,2,1,0:T(4,128)S(1)}, f32[1,1,3,4,512]{4,3,2,1,0:T(4,128)S(1)}, u32[]{:S(2)}, u32[]{:S(2)}) collective-permute-start(f32[1,1,3,4,512]{4,3,2,1,0:T(4,128)S(1)} %bitcast_select_fusion.3), channel_id=1, source_target_pairs={{0,1},{1,2},{2,3},{3,4},{4,5},{5,6},{6,7},{7,8},{8,9},{9,10},{10,1... | collective-permute-start | bytes 73736 | tf_op jit(solution)/shard_map/ppermute | solution.py:21
  260.6 5.8 collective-permute-start.5
  261.9 5.2 collective-permute-start.4
  325.0 81.6 %copy-start.7 = (s32[1,1,4,4096]{3,2,1,0:T(4,128)S(1)}, s32[1,1,4,4096]{3,2,1,0:T(4,128)}, u32[]{:S(2)}) copy-start(s32[1,1,4,4096]{3,2,1,0:T(4,128)} %param.14) | copy-start | bytes 196612
  405.3 15.1 %collective-permute-start.9 = (f32[1,1,3,4,512]{4,3,2,1,0:T(4,128)S(1)}, f32[1,1,3,4,512]{4,3,2,1,0:T(4,128)S(1)}, u32[]{:S(2)}, u32[]{:S(2)}) collective-permute-start(f32[1,1,3,4,512]{4,3,2,1,0:T(4,128)S(1)} %bitcast_select_fusion.2), channel_id=1, source_target_pairs={{16,0},{32,16},{48,32},{64,48},{80,64},{96,80},{112,96},{128,112},... | collective-permute-start | bytes 73736 | tf_op jit(solution)/shard_map/ppermute | solution.py:22
  406.6 13.8 %collective-permute-start.8 = (f32[1,1,3,4,512]{4,3,2,1,0:T(4,128)S(1)}, f32[1,1,3,4,512]{4,3,2,1,0:T(4,128)S(1)}, u32[]{:S(2)}, u32[]{:S(2)}) collective-permute-start(f32[1,1,3,4,512]{4,3,2,1,0:T(4,128)S(1)} %bitcast_select_fusion.2), channel_id=1, source_target_pairs={{0,16},{16,32},{32,48},{48,64},{64,80},{80,96},{96,112},{112,128},... | collective-permute-start | bytes 73736 | tf_op jit(solution)/shard_map/ppermute | solution.py:21
  410.9 9.5 collective-permute-start.11
  412.8 8.5 collective-permute-start.10
  599.1 15.2 %all-to-all-start.3 = ((f32[16,1,4608]{2,1,0:T(1,128)}), f32[16,1,4608]{2,1,0:T(1,128)S(1)}, u32[]{:S(2)}, u32[]{:S(2)}) async-start(f32[16,1,4608]{2,1,0:T(1,128)} %broadcast_in_dim.20), calls=%async_computation.3 | async-start | bytes 589824 | tf_op jit(solution)/shard_map/all_to_all | solution.py:46
  794.5 15.0 %collective-permute-start.15 = (f32[1,1,3,4,512]{4,3,2,1,0:T(4,128)S(1)}, f32[1,1,3,4,512]{4,3,2,1,0:T(4,128)S(1)}, u32[]{:S(2)}, u32[]{:S(2)}) collective-permute-start(f32[1,1,3,4,512]{4,3,2,1,0:T(4,128)S(1)} %bitcast_select_fusion.1), channel_id=1, source_target_pairs={{1,0},{2,1},{3,2},{4,3},{5,4},{6,5},{7,6},{8,7},{9,8},{10,9},{11,1... | collective-permute-start | bytes 73736 | tf_op jit(solution)/shard_map/ppermute | solution.py:22
  798.6 10.9 %collective-permute-start.14 = (f32[1,1,3,4,512]{4,3,2,1,0:T(4,128)S(1)}, f32[1,1,3,4,512]{4,3,2,1,0:T(4,128)S(1)}, u32[]{:S(2)}, u32[]{:S(2)}) collective-permute-start(f32[1,1,3,4,512]{4,3,2,1,0:T(4,128)S(1)} %bitcast_select_fusion.1), channel_id=1, source_target_pairs={{0,1},{1,2},{2,3},{3,4},{4,5},{5,6},{6,7},{7,8},{8,9},{9,10},{10,1... | collective-permute-start | bytes 73736 | tf_op jit(solution)/shard_map/ppermute | solution.py:21
  804.0 5.6 collective-permute-start.13
  805.3 4.9 collective-permute-start.12
  945.7 15.1 %collective-permute-start.19 = (f32[1,1,3,4,512]{4,3,2,1,0:T(4,128)S(1)}, f32[1,1,3,4,512]{4,3,2,1,0:T(4,128)S(1)}, u32[]{:S(2)}, u32[]{:S(2)}) collective-permute-start(f32[1,1,3,4,512]{4,3,2,1,0:T(4,128)S(1)} %bitcast_select_fusion), channel_id=1, source_target_pairs={{1,0},{2,1},{3,2},{4,3},{5,4},{6,5},{7,6},{8,7},{9,8},{10,9},{11,1... | collective-permute-start | bytes 73736 | tf_op jit(solution)/shard_map/ppermute | solution.py:22
  947.6 13.2 %collective-permute-start.18 = (f32[1,1,3,4,512]{4,3,2,1,0:T(4,128)S(1)}, f32[1,1,3,4,512]{4,3,2,1,0:T(4,128)S(1)}, u32[]{:S(2)}, u32[]{:S(2)}) collective-permute-start(f32[1,1,3,4,512]{4,3,2,1,0:T(4,128)S(1)} %bitcast_select_fusion), channel_id=1, source_target_pairs={{0,1},{1,2},{2,3},{3,4},{4,5},{5,6},{6,7},{7,8},{8,9},{9,10},{10,1... | collective-permute-start | bytes 73736 | tf_op jit(solution)/shard_map/ppermute | solution.py:21
  955.2 5.6 collective-permute-start.17
  956.5 5.2 collective-permute-start.16
  (7 other events, 23.3 us)
where the time goes:
time: 999 us; the launch traced here: 983 us
  other arithmetic  552 us (55%)
  local copies, waits for them, and re-layouts  267 us (27%)
  starting transfers between devices  81.4 us (8%)
  blocking collectives  54.8 us (5%)
  waiting for transfers between devices  14.7 us (1%)
  matrix products  12.7 us (1%)
    scatter-add x4, other arithmetic, element_apply(): jnp.zeros_like(field).at[:, node_index]  278 us
    gather x8, local copies, waits for them, and re-layouts, element_apply(): gathered = field[:, node_index].reshape(81, elem_count)  131 us
    scatter-add x1, other arithmetic, restrict(): return jnp.zeros((3, coarse_width), field.dtype).at[:, coarse_index].add(...  87.8 us
    scatter-add x1, other arithmetic, local(): local_diag = jnp.zeros_like(mass_here).at[:, node_index].add(main_diag[:,...  74.9 us
    scatter-add x5, other arithmetic, exchange_faces(): return field.at[:, face_index].add(received, mode='drop')  67.7 us
    ppermute x10, starting transfers between devices, with_halo(): lax.ppermute(last, axis, up)  56.2 us
    gather x1, local copies, waits for them, and re-layouts, prolong(): return jnp.sum(weights[None] * coarse_table[:, coarse_index], axis=1)  54.4 us
    gather x10, local copies, waits for them, and re-layouts, exchange_faces(): outgoing = field.at[:, face_index].get(mode='fill', fill_value=0.0)  48.6 us
  transfers between devices with their start and end apart: 21, of which 6 were waited for; matrix products, arithmetic and copies ran while one was open for 0% of the time, Pallas kernels for 0%

commit v1 on v0

v1 whole, which is shorter than its diff:
```python
import jax
import jax.numpy as jnp
from jax import lax
from jax.experimental import pallas as pl
from jax.experimental.pallas import tpu as pltpu
from jax.sharding import PartitionSpec as P

DAMPING = 0.6
MESH = pl.DeviceIdType.MESH
BF16 = jnp.bfloat16
F32 = jnp.float32
I32 = jnp.int32
NT = (((1,), (1,)), ((), ()))
NN = (((1,), (0,)), ((), ()))

ROWS = 32
NODES_PER = 27
ELEM = 512
CN = 1536
WIN = 64
RB = 288


def dot(a, b, dims):
    return lax.dot_general(a, b, dims, preferred_element_type=F32)


def dot_exact(a, b, dims):
    return lax.dot_general(
        a, b, dims, precision=lax.Precision.HIGHEST, preferred_element_type=F32
    )


def split(x):
    high = x.astype(BF16)
    low = (x - high.astype(F32)).astype(BF16)
    return high, low


def lane_gather(row, lanes):
    return jnp.take_along_axis(row, lanes, axis=1, mode="promise_in_bounds")


def pick(load_row, rows, hi, lo, fields):
    got = [jnp.zeros(hi.shape, F32) for _ in range(fields)]
    for r in range(rows):
        here = hi == r
        for c in range(fields):
            row = jnp.broadcast_to(load_row(c, r), hi.shape)
            got[c] = jnp.where(here, lane_gather(row, lo), got[c])
    return got


def kernel(
    n_grp, n_dev,
    rhs_ref, nodes_ref, coef_ref, mass_ref, face_ref, cn_ref, cw_ref, em_ref, chol_ref,
    out_ref,
    z_t, w_t, rhs_t, mass_t, dinv_t, hi_i, lo_i, gath, p_hi, p_lo, m_hl, bt, oh,
    f_hi, f_lo, v_hi, v_lo, pwh, pwl, flat,
    send, recv, s1_send, s1_recv, s2_send, s2_recv, s3_send, s3_recv, lblk,
    send_sem, recv_sem, s1_ss, s1_rs, s2_ss, s2_rs, s3_ss, s3_rs, l_sem,
):
    g = lax.axis_index("grp")
    d = lax.axis_index("dev")

    block0 = (3 * g) // 4
    block1 = lax.rem(block0 + 1, CN // 128)
    l_copies = []
    for c in range(3):
        for b, block in enumerate((block0, block1)):
            at = pl.multiple_of(CN * c + 128 * block, 128)
            copy = pltpu.make_async_copy(
                chol_ref.at[:, pl.ds(at, 128)], lblk.at[2 * c + b], l_sem.at[2 * c + b]
            )
            copy.start()
            l_copies.append(copy)

    barrier = pltpu.get_barrier_semaphore()
    for k in range(1, n_dev):
        pl.semaphore_signal(
            barrier, inc=1, device_id=(g, lax.rem(d + k, n_dev)), device_id_type=MESH
        )
    for k in range(1, n_grp):
        pl.semaphore_signal(
            barrier, inc=1, device_id=(lax.rem(g + k, n_grp), d), device_id_type=MESH
        )

    for c in range(3):
        for r in range(ROWS):
            rhs_t[c * ROWS + r : c * ROWS + r + 1, :] = rhs_ref[c : c + 1, 128 * r : 128 * r + 128]
            mass_t[c * ROWS + r : c * ROWS + r + 1, :] = mass_ref[c : c + 1, 128 * r : 128 * r + 128]
    for f in range(4):
        for r in range(4):
            face = face_ref[f : f + 1, 128 * r : 128 * r + 128]
            f_hi[4 * f + r : 4 * f + r + 1, :] = face >> 7
            f_lo[4 * f + r : 4 * f + r + 1, :] = face & 127

    hi_i[...] = jnp.zeros((32, ELEM), I32)
    lo_i[...] = jnp.zeros((32, ELEM), I32)
    hi_i[0:NODES_PER, :] = nodes_ref[...] >> 7
    lo_i[0:NODES_PER, :] = nodes_ref[...] & 127

    def one_hot(index_row, count):
        at = jnp.broadcast_to(index_row, (count, index_row.shape[1]))
        number = lax.broadcasted_iota(I32, at.shape, 0)
        return jnp.where(at == number, 1.0, 0.0).astype(BF16)

    def make_one_hot(i, carry):
        oh[i] = one_hot(hi_i[pl.ds(i, 1), :], ROWS)
        bt[i] = one_hot(lo_i[pl.ds(i, 1), :], 128)
        return carry

    lax.fori_loop(0, NODES_PER, make_one_hot, 0)

    row_of = lax.broadcasted_iota(I32, (96, 81), 0)
    col_of = lax.broadcasted_iota(I32, (96, 81), 1)
    place = (col_of == 27 * (row_of // 32) + row_of % 32) & (row_of % 32 < 27)
    place = jnp.where(place, 1.0, 0.0)
    matrix = dot_exact(dot_exact(place, em_ref[...], NN), place, NT)
    mh, ml = split(matrix)
    m_hl[0:96, :] = mh
    m_hl[96:192, :] = ml
    eye = lax.broadcasted_iota(I32, (96, 96), 0) == lax.broadcasted_iota(I32, (96, 96), 1)
    main_diag = jnp.sum(jnp.where(eye, matrix, 0.0), axis=1, keepdims=True)
    coef = coef_ref[...]

    def put_product(product):
        high = product.astype(BF16).astype(F32)
        p_hi[...] = high
        p_lo[...] = product - high

    def scatter():
        def body(i, acc):
            hot = oh[i]
            blocks = []
            for part in (p_hi, p_lo):
                for c in range(3):
                    row = part[pl.ds(c * 32 + i, 1), :]
                    value = jnp.broadcast_to(row, (ROWS, ELEM)).astype(BF16)
                    blocks.append(value * hot)
            return acc + dot(jnp.concatenate(blocks, axis=0), bt[i], NT)

        acc = lax.fori_loop(0, NODES_PER, body, jnp.zeros((192, 128), F32))
        return acc[0:96] + acc[96:192]

    acc = jnp.zeros((64, 128), F32)
    for f in range(4):
        face = face_ref[f : f + 1, :]
        hot = one_hot(face >> 7, ROWS)
        slot = lax.broadcasted_iota(I32, (ROWS, ELEM), 1) + (512 * f + 1)
        a = jnp.concatenate(
            [(slot >> 6).astype(F32).astype(BF16) * hot, (slot & 63).astype(F32).astype(BF16) * hot],
            axis=0,
        )
        acc = acc + dot(a, one_hot(face & 127, 128), NT)
    inverse = (64.0 * acc[0:32] + acc[32:64]).astype(I32) - 1
    v_hi[...] = inverse >> 7
    v_lo[...] = inverse & 127

    put_product(main_diag * coef)
    w_t[...] = mass_t[...] + scatter()

    pl.semaphore_wait(barrier, n_dev + n_grp - 2)

    up_g, down_g = lax.rem(g + 1, n_grp), lax.rem(g + n_grp - 1, n_grp)
    up_d, down_d = lax.rem(d + 1, n_dev), lax.rem(d + n_dev - 1, n_dev)
    partners = ((down_g, d), (up_g, d), (g, down_d), (g, up_d))

    def exchange(k, cover=None):
        for half in range(2):
            hi, lo = f_hi[8 * half : 8 * half + 8, :], f_lo[8 * half : 8 * half + 8, :]
            got = pick(lambda c, r: w_t[c * ROWS + r : c * ROWS + r + 1, :], ROWS, hi, lo, 3)
            for c in range(3):
                send[k, 2 * half, 4 * c : 4 * c + 4, :] = got[c][0:4]
                send[k, 2 * half + 1, 4 * c : 4 * c + 4, :] = got[c][4:8]
        copies = []
        for f in range(4):
            copy = pltpu.make_async_remote_copy(
                src_ref=send.at[k, f],
                dst_ref=recv.at[k, f ^ 1],
                send_sem=send_sem.at[k, f],
                recv_sem=recv_sem.at[k, f ^ 1],
                device_id=partners[f],
                device_id_type=MESH,
            )
            copy.start()
            copies.append(copy)
        if cover is not None:
            cover()
        for f in range(4):
            copies[f].wait()
        for q in range(4):
            hi, lo = v_hi[8 * q : 8 * q + 8, :], v_lo[8 * q : 8 * q + 8, :]
            got = pick(
                lambda c, r: recv[k, r // 4, 4 * c + r % 4 : 4 * c + r % 4 + 1, :], 16, hi, lo, 3
            )
            for c in range(3):
                at = slice(c * ROWS + 8 * q, c * ROWS + 8 * q + 8)
                w_t[at, :] = w_t[at, :] + got[c]

    def operate(k):
        def body(v, carry):
            row = pl.multiple_of(8 * (v // 4), 8)
            lane = pl.multiple_of(128 * (v % 4), 128)
            hi, lo = hi_i[pl.ds(row, 8), pl.ds(lane, 128)], lo_i[pl.ds(row, 8), pl.ds(lane, 128)]
            got = pick(lambda c, r: z_t[c * ROWS + r : c * ROWS + r + 1, :], ROWS, hi, lo, 3)
            for c in range(3):
                gath[pl.ds(row + 32 * c, 8), pl.ds(lane, 128)] = got[c]
            return carry

        lax.fori_loop(0, 16, body, 0)
        gh, gl = split(gath[...])
        both = dot(m_hl[...], gh, NN)
        product = both[0:96] + both[96:192] + dot(m_hl[0:96, :], gl, NN)
        put_product(product * coef)
        w_t[...] = mass_t[...] * z_t[...] + scatter()
        exchange(k)

    def make_interpolation():
        home = 6 * (n_dev * g + d)

        def body(q, carry):
            at = pl.ds(pl.multiple_of(512 * q, 512), 512)
            number = lax.broadcasted_iota(I32, (WIN, 512), 0)
            total = jnp.zeros((WIN, 512), F32)
            for j in range(4):
                rel = cn_ref[j : j + 1, at] - home
                rel = jnp.where(rel < 0, rel + CN, rel)
                hit = jnp.broadcast_to(rel, (WIN, 512)) == number
                total = total + jnp.where(hit, jnp.broadcast_to(cw_ref[j : j + 1, at], (WIN, 512)), 0.0)
            high, low = split(total)
            pwh[:, at] = high
            pwl[:, at] = low
            return carry

        lax.fori_loop(0, 8, body, 0)

    exchange(0, make_interpolation)
    dinv_t[...] = DAMPING / w_t[...]
    z_t[...] = rhs_t[...] * dinv_t[...]
    operate(1)
    z_t[...] = z_t[...] + (rhs_t[...] - w_t[...]) * dinv_t[...]
    operate(2)

    w_t[...] = rhs_t[...] - w_t[...]
    flat[...] = jnp.zeros((8, 4096), F32)
    for c in range(3):
        for r in range(ROWS):
            flat[c : c + 1, 128 * r : 128 * r + 128] = w_t[c * ROWS + r : c * ROWS + r + 1, :]
    rh, rl = split(flat[0:8, :])
    left = jnp.concatenate([rh, rl], axis=0)
    first = dot(left, pwh[...], NT)
    window = first[0:8] + first[8:16] + dot(rh, pwl[...], NT)
    offset = 96 * g - 128 * block0 + 6 * d
    shift = lax.broadcasted_iota(I32, (WIN, 256), 1) == lax.broadcasted_iota(I32, (WIN, 256), 0) + offset
    shift = jnp.where(shift, 1.0, 0.0)
    s1_send[...] = dot_exact(window, shift, NN)[0:4]

    def to_all(src, dst, send_sems, recv_sems, along_dev):
        copies = []
        for k in range(1, n_dev if along_dev else n_grp):
            if along_dev:
                target, slot = (g, lax.rem(d + k, n_dev)), k
            else:
                target, slot = (lax.rem(g + k, n_grp), d), k
            copy = pltpu.make_async_remote_copy(
                src_ref=src,
                dst_ref=dst.at[slot],
                send_sem=send_sems.at[k],
                recv_sem=recv_sems.at[k],
                device_id=target,
                device_id_type=MESH,
            )
            copy.start()
            copies.append(copy)
        for copy in copies:
            copy.wait()

    to_all(s1_send, s1_recv, s1_ss, s1_rs, True)
    span = s1_send[...]
    for k in range(1, n_dev):
        span = span + s1_recv[k]
    for copy in l_copies:
        copy.wait()
    acc = jnp.zeros((RB, 128), F32)
    for c in range(3):
        for b in range(2):
            acc = acc + lblk[2 * c + b] * span[c : c + 1, 128 * b : 128 * b + 128]
    s2_send[...] = dot_exact(jnp.ones((8, 128), F32), acc, NT)[0:1]
    to_all(s2_send, s2_recv, s2_ss, s2_rs, False)
    halfway = s2_send[...]
    for k in range(1, n_grp):
        halfway = halfway + s2_recv[k]
    halfway = jnp.broadcast_to(halfway, (8, RB))
    for c in range(3):
        for b in range(2):
            term = dot_exact(halfway, lblk[2 * c + b], NN)
            s3_send[c : c + 1, 128 * b : 128 * b + 128] = term[0:1]
    s3_send[3:4, :] = jnp.zeros((1, 256), F32)
    to_all(s3_send, s3_recv, s3_ss, s3_rs, True)
    span = s3_send[...]
    for k in range(1, n_dev):
        span = span + s3_recv[k]
    correction = dot_exact(jnp.concatenate([span, span], axis=0), shift, NT)
    ch, cl = split(correction)
    left = jnp.concatenate([ch, cl], axis=0)
    first = dot(left, pwh[...], NN)
    flat[0:8, :] = first[0:8] + first[8:16] + dot(ch, pwl[...], NN)
    for c in range(3):
        for r in range(ROWS):
            at = slice(c * ROWS + r, c * ROWS + r + 1)
            z_t[at, :] = z_t[at, :] + flat[c : c + 1, 128 * r : 128 * r + 128]

    operate(3)
    z_t[...] = z_t[...] + (rhs_t[...] - w_t[...]) * dinv_t[...]
    operate(4)
    z_t[...] = z_t[...] + (rhs_t[...] - w_t[...]) * dinv_t[...]
    for c in range(3):
        for r in range(ROWS):
            out_ref[c : c + 1, 128 * r : 128 * r + 128] = z_t[c * ROWS + r : c * ROWS + r + 1, :]


def solution(mesh):
    n_grp, n_dev = mesh.shape["grp"], mesh.shape["dev"]

    def local(rhs, nodes, coef, mass, faces, coarse, weights, matrix, chol):
        vmem = pl.BlockSpec(memory_space=pltpu.VMEM)
        dma = pltpu.SemaphoreType.DMA

        def body(*refs):
            kernel(n_grp, n_dev, *refs)

        out = pl.pallas_call(
            body,
            name="two_level",
            out_shape=jax.ShapeDtypeStruct((3, 4096), F32),
            in_specs=[vmem] * 8 + [pl.BlockSpec(memory_space=pl.ANY)],
            out_specs=vmem,
            scratch_shapes=[
                pltpu.VMEM((96, 128), F32),
                pltpu.VMEM((96, 128), F32),
                pltpu.VMEM((96, 128), F32),
                pltpu.VMEM((96, 128), F32),
                pltpu.VMEM((96, 128), F32),
                pltpu.VMEM((32, ELEM), I32),
                pltpu.VMEM((32, ELEM), I32),
                pltpu.VMEM((96, ELEM), F32),
                pltpu.VMEM((96, ELEM), F32),
                pltpu.VMEM((96, ELEM), F32),
                pltpu.VMEM((192, 96), BF16),
                pltpu.VMEM((NODES_PER, 128, ELEM), BF16),
                pltpu.VMEM((NODES_PER, ROWS, ELEM), BF16),
                pltpu.VMEM((16, 128), I32),
                pltpu.VMEM((16, 128), I32),
                pltpu.VMEM((32, 128), I32),
                pltpu.VMEM((32, 128), I32),
                pltpu.VMEM((WIN, 4096), BF16),
                pltpu.VMEM((WIN, 4096), BF16),
                pltpu.VMEM((8, 4096), F32),
                pltpu.VMEM((5, 4, 16, 128), F32),
                pltpu.VMEM((5, 4, 16, 128), F32),
                pltpu.VMEM((4, 256), F32),
                pltpu.VMEM((n_dev, 4, 256), F32),
                pltpu.VMEM((1, RB), F32),
                pltpu.VMEM((n_grp, 1, RB), F32),
                pltpu.VMEM((4, 256), F32),
                pltpu.VMEM((n_dev, 4, 256), F32),
                pltpu.VMEM((6, RB, 128), F32),
                dma((5, 4)), dma((5, 4)),
                dma((n_dev,)), dma((n_dev,)),
                dma((n_grp,)), dma((n_grp,)),
                dma((n_dev,)), dma((n_dev,)),
                dma((6,)),
            ],
            compiler_params=pltpu.CompilerParams(
                collective_id=0, has_side_effects=True, vmem_limit_bytes=48 << 20
            ),
        )(
            rhs[0, 0], nodes[0, 0], coef[0], mass[0, 0], faces[0, 0], coarse[0, 0],
            weights[0, 0], matrix, chol,
        )
        return out[None, None]

    return jax.shard_map(
        local,
        mesh=mesh,
        in_specs=(
            P("grp", "dev", None, None),
            P("grp", "dev", None, None),
            P("grp", "dev", None),
            P("grp", "dev", None, None),
            P("grp", "dev", None, None),
            P("grp", "dev", None, None),
            P("grp", "dev", None, None),
            P(),
            P("dev", None),
        ),
        out_specs=P("grp", "dev", None, None),
        check_vma=False,
    )
```

time: 999 us -> 107 us (0.11); the launches traced: 983 us -> 106 us
  other arithmetic: 552 us -> 0 us
  local copies, waits for them, and re-layouts: 267 us -> 8.72 us
  Pallas kernels: 0 us -> 97.7 us
  starting transfers between devices: 81.4 us -> 0 us
  blocking collectives: 54.8 us -> 0 us
  waiting for transfers between devices: 14.7 us -> 0 us
  matrix products: 12.7 us -> 0 us
    scatter-add x11 -> x0, other arithmetic: 509 us -> none  [the longest x4 278 us: element_apply(): jnp.zeros_like(field).at[:, node_index]]
    gather x20 -> x0, local copies, waits for them, and re-layouts: 235 us -> none  [the longest x8 131 us: element_apply(): gathered = field[:, node_index].reshape(81, elem_count)]
    pallas_call x0 -> x1, Pallas kernels: none -> 97.7 us  [local(): pl.pallas_call(body, name='two_level', out_shape=jax.ShapeDtypeStruct((3,...]
    ppermute x20 -> x0, starting transfers between devices: 77.6 us -> none  [the longest x10 56.2 us: with_halo(): lax.ppermute(last, axis, up)]
    all_to_all x3 -> x0, blocking collectives: 54.8 us -> none  [the longest x2 32.1 us: from_everyone(): lax.all_to_all(jnp.broadcast_to(value[None], (length, *value.shape)), axi...]
    mul x5 -> x0, other arithmetic: 23 us -> none  [the longest x3 14.2 us: element_apply(): return summed + mass_here * field]
    reshape x15 -> x0, local copies, waits for them, and re-layouts: 17.3 us -> none  [the longest x8 16.8 us: element_apply(): product.reshape(3, 27, elem_count)]
    dot_general x6 -> x0, matrix products: 12.7 us -> none  [the longest x1 6.09 us: local(): jnp.dot(chol_inverse, collect(slice_sum, 'dev', 0), precision=PRECISE)]
  transfers between devices with their start and end apart: 21 -> 0, of which waited for: 6 -> 0; matrix products, arithmetic and copies ran while one was open for 0% -> 0% of each run, Pallas kernels for 0% -> 0%
where the time goes in v1:
time: 107 us; the launch traced here: 106 us
  Pallas kernels  97.7 us (91%)
  local copies, waits for them, and re-layouts  8.72 us (8%)
    pallas_call x1, Pallas kernels, local(): pl.pallas_call(body, name='two_level', out_shape=jax.ShapeDtypeStruct((3,...  97.7 us
    unnamed x14, local copies, waits for them, and re-layouts  8.05 us

profile of v1, /device:TPU:1, one launch (start us, length us, event | category | flops | bytes accessed | tf_op | source)
XLA Modules:
  0.0 106.4 jit_solution(10235248452802205151)
XLA Ops:
  0.0 0.8 copy.17
  0.8 0.9 copy_bitcast_fusion
  1.7 0.0 copy-start
  1.7 2.5 %copy-done = f32[288,4608]{1,0:T(8,128)S(1)} copy-done((f32[288,4608]{1,0:T(8,128)S(1)}, f32[288,4608]{1,0:T(8,128)}, u32[]{:S(2)}) %copy-start) | copy-done | bytes 5308440
  4.2 0.0 copy-start.1
  4.2 0.8 copy-done.1
  5.1 0.0 copy-start.2
  5.1 0.8 copy-done.2
  5.9 0.0 copy-start.3
  5.9 0.8 copy-done.3
  6.7 0.0 copy-start.4
  6.7 0.7 copy-done.4
  7.4 0.0 copy-start.5
  7.4 0.7 copy-done.5
  8.1 97.7 %two_level.1 = f32[3,4096]{1,0:T(4,128)S(1)} custom-call(f32[3,4096]{1,0:T(4,128)S(1)} %get-tuple-element.6.refs_0_, s32[27,512]{1,0:T(8,128)S(1)} %bitcast.13, f32[1,512]{1,0:T(1,128)S(1)} %bitcast.17, f32[3,4096]{1,0:T(4,128)S(1)} %get-tuple-element.5.refs_3_, s32[4,512]{1,0:T(4,128)S(1)} %bitcast.16, s32[4,4096]{1,0:T(4,128)S(1)} %bitcast.14, ...), custom_call_target="tpu_custom_call" | custom-call | tf_op jit(solution)/shard_map/two_level/pallas_call | solution.py:333
  105.7 0.7 copy.10
Async XLA Ops:
  1.7 2.5 %copy-start = (f32[288,4608]{1,0:T(8,128)S(1)}, f32[288,4608]{1,0:T(8,128)}, u32[]{:S(2)}) copy-start(f32[288,4608]{1,0:T(8,128)} %refs_8_.1) | copy-start | bytes 15925252
  4.2 0.8 copy-start.1
  5.1 0.8 copy-start.2
  5.9 0.8 copy-start.3
  6.7 0.7 copy-start.4
  7.4 0.7 copy-start.5

commit v2 on v1

--- a/solution.py
+++ b/solution.py
@@ -53,15 +53,24 @@
 
 def kernel(
     n_grp, n_dev,
-    rhs_ref, nodes_ref, coef_ref, mass_ref, face_ref, cn_ref, cw_ref, em_ref, chol_ref,
+    rhs_hbm, nodes_hbm, coef_hbm, mass_hbm, face_hbm, cn_hbm, cw_hbm, em_hbm, chol_ref,
     out_ref,
     z_t, w_t, rhs_t, mass_t, dinv_t, hi_i, lo_i, gath, p_hi, p_lo, m_hl, bt, oh,
     f_hi, f_lo, v_hi, v_lo, pwh, pwl, flat,
+    nodes_ref, coef_ref, face_ref, cn_ref, cw_ref, em_ref,
     send, recv, s1_send, s1_recv, s2_send, s2_recv, s3_send, s3_recv, lblk,
-    send_sem, recv_sem, s1_ss, s1_rs, s2_ss, s2_rs, s3_ss, s3_rs, l_sem,
+    send_sem, recv_sem, s1_ss, s1_rs, s2_ss, s2_rs, s3_ss, s3_rs, l_sem, in_sem,
 ):
     g = lax.axis_index("grp")
     d = lax.axis_index("dev")
+
+    pairs = (
+        (nodes_hbm, nodes_ref), (face_hbm, face_ref), (em_hbm, em_ref), (coef_hbm, coef_ref),
+        (mass_hbm, mass_t), (rhs_hbm, rhs_t), (cn_hbm, cn_ref), (cw_hbm, cw_ref),
+    )
+    loads = [pltpu.make_async_copy(a, b, in_sem.at[j]) for j, (a, b) in enumerate(pairs)]
+    for load in loads:
+        load.start()
 
     block0 = (3 * g) // 4
     block1 = lax.rem(block0 + 1, CN // 128)
@@ -85,10 +94,8 @@
             barrier, inc=1, device_id=(lax.rem(g + k, n_grp), d), device_id_type=MESH
         )
 
-    for c in range(3):
-        for r in range(ROWS):
-            rhs_t[c * ROWS + r : c * ROWS + r + 1, :] = rhs_ref[c : c + 1, 128 * r : 128 * r + 128]
-            mass_t[c * ROWS + r : c * ROWS + r + 1, :] = mass_ref[c : c + 1, 128 * r : 128 * r + 128]
+    for load in loads:
+        load.wait()
     for f in range(4):
         for r in range(4):
             face = face_ref[f : f + 1, 128 * r : 128 * r + 128]
@@ -97,8 +104,11 @@
 
     hi_i[...] = jnp.zeros((32, ELEM), I32)
     lo_i[...] = jnp.zeros((32, ELEM), I32)
-    hi_i[0:NODES_PER, :] = nodes_ref[...] >> 7
-    lo_i[0:NODES_PER, :] = nodes_ref[...] & 127
+    for i in range(NODES_PER):
+        for k in range(4):
+            index = nodes_ref[i, k : k + 1, :]
+            hi_i[i : i + 1, 128 * k : 128 * k + 128] = index >> 7
+            lo_i[i : i + 1, 128 * k : 128 * k + 128] = index & 127
 
     def one_hot(index_row, count):
         at = jnp.broadcast_to(index_row, (count, index_row.shape[1]))
@@ -107,7 +117,7 @@
 
     def make_one_hot(i, carry):
         oh[i] = one_hot(hi_i[pl.ds(i, 1), :], ROWS)
-        bt[i] = one_hot(lo_i[pl.ds(i, 1), :], 128)
+        bt[:, pl.ds(pl.multiple_of(ELEM * i, ELEM), ELEM)] = one_hot(lo_i[pl.ds(i, 1), :], 128)
         return carry
 
     lax.fori_loop(0, NODES_PER, make_one_hot, 0)
@@ -130,17 +140,17 @@
         p_lo[...] = product - high
 
     def scatter():
-        def body(i, acc):
+        columns = []
+        for i in range(NODES_PER):
             hot = oh[i]
             blocks = []
             for part in (p_hi, p_lo):
                 for c in range(3):
-                    row = part[pl.ds(c * 32 + i, 1), :]
+                    row = part[c * 32 + i : c * 32 + i + 1, :]
                     value = jnp.broadcast_to(row, (ROWS, ELEM)).astype(BF16)
                     blocks.append(value * hot)
-            return acc + dot(jnp.concatenate(blocks, axis=0), bt[i], NT)
-
-        acc = lax.fori_loop(0, NODES_PER, body, jnp.zeros((192, 128), F32))
+            columns.append(jnp.concatenate(blocks, axis=0))
+        acc = dot(jnp.concatenate(columns, axis=1), bt[...], NT)
         return acc[0:96] + acc[96:192]
 
     acc = jnp.zeros((64, 128), F32)
@@ -171,8 +181,8 @@
             hi, lo = f_hi[8 * half : 8 * half + 8, :], f_lo[8 * half : 8 * half + 8, :]
             got = pick(lambda c, r: w_t[c * ROWS + r : c * ROWS + r + 1, :], ROWS, hi, lo, 3)
             for c in range(3):
-                send[k, 2 * half, 4 * c : 4 * c + 4, :] = got[c][0:4]
-                send[k, 2 * half + 1, 4 * c : 4 * c + 4, :] = got[c][4:8]
+                send[k, 2 * half, c] = got[c][0:4]
+                send[k, 2 * half + 1, c] = got[c][4:8]
         copies = []
         for f in range(4):
             copy = pltpu.make_async_remote_copy(
@@ -192,7 +202,7 @@
         for q in range(4):
             hi, lo = v_hi[8 * q : 8 * q + 8, :], v_lo[8 * q : 8 * q + 8, :]
             got = pick(
-                lambda c, r: recv[k, r // 4, 4 * c + r % 4 : 4 * c + r % 4 + 1, :], 16, hi, lo, 3
+                lambda c, r: recv[k, r // 4, c, r % 4 : r % 4 + 1, :], 16, hi, lo, 3
             )
             for c in range(3):
                 at = slice(c * ROWS + 8 * q, c * ROWS + 8 * q + 8)
@@ -208,7 +218,7 @@
                 gath[pl.ds(row + 32 * c, 8), pl.ds(lane, 128)] = got[c]
             return carry
 
-        lax.fori_loop(0, 16, body, 0)
+        lax.fori_loop(0, 16, body, 0, unroll=4)
         gh, gl = split(gath[...])
         both = dot(m_hl[...], gh, NN)
         product = both[0:96] + both[96:192] + dot(m_hl[0:96, :], gl, NN)
@@ -251,24 +261,24 @@
     left = jnp.concatenate([rh, rl], axis=0)
     first = dot(left, pwh[...], NT)
     window = first[0:8] + first[8:16] + dot(rh, pwl[...], NT)
-    offset = 96 * g - 128 * block0 + 6 * d
-    shift = lax.broadcasted_iota(I32, (WIN, 256), 1) == lax.broadcasted_iota(I32, (WIN, 256), 0) + offset
-    shift = jnp.where(shift, 1.0, 0.0)
-    s1_send[...] = dot_exact(window, shift, NN)[0:4]
+    for c in range(3):
+        s1_send[:, WIN * c : WIN * c + WIN] = window[c : c + 1]
+    s1_send[:, 3 * WIN :] = jnp.zeros((1, 256 - 3 * WIN), F32)
+    s1_recv[d] = s1_send[...]
+    lane = lax.broadcasted_iota(I32, (n_dev, 128), 1)
+    first_at = 6 * lax.broadcasted_iota(I32, (n_dev, 128), 0) + (96 * g - 128 * block0)
 
     def to_all(src, dst, send_sems, recv_sems, along_dev):
+        me, count = (d, n_dev) if along_dev else (g, n_grp)
         copies = []
-        for k in range(1, n_dev if along_dev else n_grp):
-            if along_dev:
-                target, slot = (g, lax.rem(d + k, n_dev)), k
-            else:
-                target, slot = (lax.rem(g + k, n_grp), d), k
+        for k in range(1, count):
+            peer = lax.rem(me + k, count)
             copy = pltpu.make_async_remote_copy(
-                src_ref=src,
-                dst_ref=dst.at[slot],
+                src_ref=src(peer),
+                dst_ref=dst.at[me],
                 send_sem=send_sems.at[k],
                 recv_sem=recv_sems.at[k],
-                device_id=target,
+                device_id=(g, peer) if along_dev else (peer, d),
                 device_id_type=MESH,
             )
             copy.start()
@@ -276,32 +286,47 @@
         for copy in copies:
             copy.wait()
 
-    to_all(s1_send, s1_recv, s1_ss, s1_rs, True)
-    span = s1_send[...]
-    for k in range(1, n_dev):
-        span = span + s1_recv[k]
+    to_all(lambda peer: s1_send, s1_recv, s1_ss, s1_rs, True)
+    windows = s1_recv[:, 0, :]
+    span = []
+    for c in range(3):
+        row = []
+        for b in range(2):
+            at = lane + 128 * b - first_at
+            inside = (at >= 0) & (at < WIN)
+            at = jnp.where(inside, at, 0) + WIN * (c % 2)
+            values = lane_gather(windows[:, 128 * (c // 2) : 128 * (c // 2) + 128], at)
+            row.append(jnp.sum(jnp.where(inside, values, 0.0), axis=0, keepdims=True))
+        span.append(row)
     for copy in l_copies:
         copy.wait()
     acc = jnp.zeros((RB, 128), F32)
     for c in range(3):
         for b in range(2):
-            acc = acc + lblk[2 * c + b] * span[c : c + 1, 128 * b : 128 * b + 128]
+            acc = acc + lblk[2 * c + b] * span[c][b]
     s2_send[...] = dot_exact(jnp.ones((8, 128), F32), acc, NT)[0:1]
-    to_all(s2_send, s2_recv, s2_ss, s2_rs, False)
-    halfway = s2_send[...]
-    for k in range(1, n_grp):
-        halfway = halfway + s2_recv[k]
+    s2_recv[g] = s2_send[...]
+    to_all(lambda peer: s2_send, s2_recv, s2_ss, s2_rs, False)
+    halfway = jnp.sum(s2_recv[:, 0, :], axis=0, keepdims=True)
     halfway = jnp.broadcast_to(halfway, (8, RB))
-    for c in range(3):
+    parts = []
+    for c in range(3):
+        at = jnp.where(lane < WIN, lane, lane - WIN) + first_at
+        values = []
         for b in range(2):
-            term = dot_exact(halfway, lblk[2 * c + b], NN)
-            s3_send[c : c + 1, 128 * b : 128 * b + 128] = term[0:1]
-    s3_send[3:4, :] = jnp.zeros((1, 256), F32)
-    to_all(s3_send, s3_recv, s3_ss, s3_rs, True)
-    span = s3_send[...]
-    for k in range(1, n_dev):
-        span = span + s3_recv[k]
-    correction = dot_exact(jnp.concatenate([span, span], axis=0), shift, NT)
+            row = dot_exact(halfway, lblk[2 * c + b], NN)[0:1]
+            values.append(
+                lane_gather(jnp.broadcast_to(row, (n_dev, 128)), jnp.clip(at - 128 * b, 0, 127))
+            )
+        parts.append(jnp.where(at < 128, values[0], values[1]))
+    s3_send[:, 0, 0:128] = jnp.where(lane < WIN, parts[0], parts[1])
+    s3_send[:, 0, 128:256] = parts[2]
+    s3_recv[d] = s3_send[d]
+    to_all(lambda peer: s3_send.at[peer], s3_recv, s3_ss, s3_rs, True)
+    total = jnp.sum(s3_recv[:, 0, :], axis=0, keepdims=True)
+    correction = jnp.concatenate(
+        [total[:, WIN * c : WIN * c + WIN] for c in range(3)] + [jnp.zeros((5, WIN), F32)], axis=0
+    )
     ch, cl = split(correction)
     left = jnp.concatenate([ch, cl], axis=0)
     first = dot(left, pwh[...], NN)
@@ -314,17 +339,13 @@
     operate(3)
     z_t[...] = z_t[...] + (rhs_t[...] - w_t[...]) * dinv_t[...]
     operate(4)
-    z_t[...] = z_t[...] + (rhs_t[...] - w_t[...]) * dinv_t[...]
-    for c in range(3):
-        for r in range(ROWS):
-            out_ref[c : c + 1, 128 * r : 128 * r + 128] = z_t[c * ROWS + r : c * ROWS + r + 1, :]
+    out_ref[...] = z_t[...] + (rhs_t[...] - w_t[...]) * dinv_t[...]
 
 
 def solution(mesh):
     n_grp, n_dev = mesh.shape["grp"], mesh.shape["dev"]
 
     def local(rhs, nodes, coef, mass, faces, coarse, weights, matrix, chol):
-        vmem = pl.BlockSpec(memory_space=pltpu.VMEM)
         dma = pltpu.SemaphoreType.DMA
 
         def body(*refs):
@@ -333,9 +354,9 @@
         out = pl.pallas_call(
             body,
             name="two_level",
-            out_shape=jax.ShapeDtypeStruct((3, 4096), F32),
-            in_specs=[vmem] * 8 + [pl.BlockSpec(memory_space=pl.ANY)],
-            out_specs=vmem,
+            out_shape=jax.ShapeDtypeStruct((96, 128), F32),
+            in_specs=[pl.BlockSpec(memory_space=pltpu.HBM)] * 9,
+            out_specs=pl.BlockSpec(memory_space=pltpu.VMEM),
             scratch_shapes=[
                 pltpu.VMEM((96, 128), F32),
                 pltpu.VMEM((96, 128), F32),
@@ -348,7 +369,7 @@
                 pltpu.VMEM((96, ELEM), F32),
                 pltpu.VMEM((96, ELEM), F32),
                 pltpu.VMEM((192, 96), BF16),
-                pltpu.VMEM((NODES_PER, 128, ELEM), BF16),
+                pltpu.VMEM((128, NODES_PER * ELEM), BF16),
                 pltpu.VMEM((NODES_PER, ROWS, ELEM), BF16),
                 pltpu.VMEM((16, 128), I32),
                 pltpu.VMEM((16, 128), I32),
@@ -357,29 +378,36 @@
                 pltpu.VMEM((WIN, 4096), BF16),
                 pltpu.VMEM((WIN, 4096), BF16),
                 pltpu.VMEM((8, 4096), F32),
-                pltpu.VMEM((5, 4, 16, 128), F32),
-                pltpu.VMEM((5, 4, 16, 128), F32),
-                pltpu.VMEM((4, 256), F32),
-                pltpu.VMEM((n_dev, 4, 256), F32),
+                pltpu.VMEM((27, 4, 128), I32),
+                pltpu.VMEM((1, ELEM), F32),
+                pltpu.VMEM((4, 512), I32),
+                pltpu.VMEM((4, 4096), I32),
+                pltpu.VMEM((4, 4096), F32),
+                pltpu.VMEM((81, 81), F32),
+                pltpu.VMEM((5, 4, 3, 4, 128), F32),
+                pltpu.VMEM((5, 4, 3, 4, 128), F32),
+                pltpu.VMEM((1, 256), F32),
+                pltpu.VMEM((n_dev, 1, 256), F32),
                 pltpu.VMEM((1, RB), F32),
                 pltpu.VMEM((n_grp, 1, RB), F32),
-                pltpu.VMEM((4, 256), F32),
-                pltpu.VMEM((n_dev, 4, 256), F32),
+                pltpu.VMEM((n_dev, 1, 256), F32),
+                pltpu.VMEM((n_dev, 1, 256), F32),
                 pltpu.VMEM((6, RB, 128), F32),
                 dma((5, 4)), dma((5, 4)),
                 dma((n_dev,)), dma((n_dev,)),
                 dma((n_grp,)), dma((n_grp,)),
                 dma((n_dev,)), dma((n_dev,)),
                 dma((6,)),
+                dma((8,)),
             ],
             compiler_params=pltpu.CompilerParams(
-                collective_id=0, has_side_effects=True, vmem_limit_bytes=48 << 20
+                collective_id=0, has_side_effects=True, vmem_limit_bytes=67_000_000
             ),
         )(
-            rhs[0, 0], nodes[0, 0], coef[0], mass[0, 0], faces[0, 0], coarse[0, 0],
-            weights[0, 0], matrix, chol,
+            rhs.reshape(96, 128), nodes.reshape(27, 4, 128), coef[0], mass.reshape(96, 128),
+            faces[0, 0], coarse[0, 0], weights[0, 0], matrix, chol,
         )
-        return out[None, None]
+        return out.reshape(1, 1, 3, 4096)
 
     return jax.shard_map(
         local,

time: 107 us -> 75.7 us (0.71)
  Pallas kernels: 97.7 us -> 73.9 us
  local copies, waits for them, and re-layouts: 8.72 us -> 1.42 us
    pallas_call x1, Pallas kernels: 97.7 us -> 73.9 us  [local(): pl.pallas_call(body, name='two_level', out_shape=jax.ShapeDtypeStruct((96...]
    unnamed x14 -> x1, local copies, waits for them, and re-layouts: 8.05 us -> 1.42 us
where the time goes in v2:
time: 75.7 us; the launch traced here: 75.3 us
  Pallas kernels  73.9 us (98%)
  local copies, waits for them, and re-layouts  1.42 us (2%)
    pallas_call x1, Pallas kernels, local(): pl.pallas_call(body, name='two_level', out_shape=jax.ShapeDtypeStruct((96...  73.9 us

profile of v2, /device:TPU:1, one launch (start us, length us, event | category | flops | bytes accessed | tf_op | source)
XLA Modules:
  0.0 75.3 jit_solution(16836194533858870767)
XLA Ops:
  0.0 73.9 %two_level.1 = f32[96,128]{1,0:T(8,128)} custom-call(f32[96,128]{1,0:T(8,128)} %bitcast.12, s32[27,4,128]{2,1,0:T(4,128)} %bitcast.11, f32[1,512]{1,0:T(1,128)} %bitcast.15, f32[96,128]{1,0:T(8,128)} %bitcast.13, s32[4,512]{1,0:T(4,128)} %bitcast.14, s32[4,4096]{1,0:T(4,128)} %bitcast.9, f32[4,4096]{1,0:T(4,128)} %bitcast.10, f32[81,81]{1,0:T(8,128)} %refs_7_.1, ...), custom_call_target="tpu_custom_call" | custom-call | tf_op jit(solution)/shard_map/two_level/pallas_call | solution.py:354
  73.9 1.4 %copy.13 = f32[1,1,3,4096]{3,1,2,0:T(1,128)} copy(f32[1,1,3,4096]{3,1,2,0:T(1,128)} %bitcast.8) | data formatting | bytes 98304

commit v3 on v2

--- a/solution.py
+++ b/solution.py
@@ -14,6 +14,7 @@
 NN = (((1,), (0,)), ((), ()))
 
 ROWS = 32
+FROWS = 16
 NODES_PER = 27
 ELEM = 512
 CN = 1536
@@ -41,8 +42,9 @@
     return jnp.take_along_axis(row, lanes, axis=1, mode="promise_in_bounds")
 
 
-def pick(load_row, rows, hi, lo, fields):
-    got = [jnp.zeros(hi.shape, F32) for _ in range(fields)]
+def pick(load_row, rows, hi, lo, start):
+    got = list(start)
+    fields = len(got)
     for r in range(rows):
         here = hi == r
         for c in range(fields):
@@ -55,8 +57,9 @@
     n_grp, n_dev,
     rhs_hbm, nodes_hbm, coef_hbm, mass_hbm, face_hbm, cn_hbm, cw_hbm, em_hbm, chol_ref,
     out_ref,
-    z_t, w_t, rhs_t, mass_t, dinv_t, hi_i, lo_i, gath, p_hi, p_lo, m_hl, bt, oh,
-    f_hi, f_lo, v_hi, v_lo, pwh, pwl, flat,
+    zf, zi, wf, wi, rf, ri, mf, mi, df, di,
+    hi_i, lo_i, gath, p_hi, p_lo, m_hl, bn, oh,
+    f_hi, f_lo, v_hi, v_lo, inv_t, pwh, pwl, flat,
     nodes_ref, coef_ref, face_ref, cn_ref, cw_ref, em_ref,
     send, recv, s1_send, s1_recv, s2_send, s2_recv, s3_send, s3_recv, lblk,
     send_sem, recv_sem, s1_ss, s1_rs, s2_ss, s2_rs, s3_ss, s3_rs, l_sem, in_sem,
@@ -66,7 +69,7 @@
 
     pairs = (
         (nodes_hbm, nodes_ref), (face_hbm, face_ref), (em_hbm, em_ref), (coef_hbm, coef_ref),
-        (mass_hbm, mass_t), (rhs_hbm, rhs_t), (cn_hbm, cn_ref), (cw_hbm, cw_ref),
+        (mass_hbm, mi), (rhs_hbm, ri), (cn_hbm, cn_ref), (cw_hbm, cw_ref),
     )
     loads = [pltpu.make_async_copy(a, b, in_sem.at[j]) for j, (a, b) in enumerate(pairs)]
     for load in loads:
@@ -102,6 +105,26 @@
             f_hi[4 * f + r : 4 * f + r + 1, :] = face >> 7
             f_lo[4 * f + r : 4 * f + r + 1, :] = face & 127
 
+    def one_hot(index_row, count):
+        at = jnp.broadcast_to(index_row, (count, index_row.shape[1]))
+        number = lax.broadcasted_iota(I32, at.shape, 0)
+        return jnp.where(at == number, 1.0, 0.0).astype(BF16)
+
+    acc = jnp.zeros((64, 128), F32)
+    for f in range(4):
+        face = face_ref[f : f + 1, :]
+        hot = one_hot(face >> 7, ROWS)
+        slot = lax.broadcasted_iota(I32, (ROWS, ELEM), 1) + (512 * f + 1)
+        a = jnp.concatenate(
+            [(slot >> 6).astype(F32).astype(BF16) * hot, (slot & 63).astype(F32).astype(BF16) * hot],
+            axis=0,
+        )
+        acc = acc + dot(a, one_hot(face & 127, 128), NT)
+    inverse = (64.0 * acc[0:32] + acc[32:64]).astype(I32) - 1
+    inv_t[...] = inverse
+    v_hi[...] = inverse >> 7
+    v_lo[...] = inverse & 127
+
     hi_i[...] = jnp.zeros((32, ELEM), I32)
     lo_i[...] = jnp.zeros((32, ELEM), I32)
     for i in range(NODES_PER):
@@ -110,17 +133,38 @@
             hi_i[i : i + 1, 128 * k : 128 * k + 128] = index >> 7
             lo_i[i : i + 1, 128 * k : 128 * k + 128] = index & 127
 
-    def one_hot(index_row, count):
-        at = jnp.broadcast_to(index_row, (count, index_row.shape[1]))
-        number = lax.broadcasted_iota(I32, at.shape, 0)
-        return jnp.where(at == number, 1.0, 0.0).astype(BF16)
+    def renumber(v, carry):
+        row = pl.multiple_of(8 * (v // 4), 8)
+        lane = pl.multiple_of(128 * (v % 4), 128)
+        at = (pl.ds(row, 8), pl.ds(lane, 128))
+        hi, lo = hi_i[at], lo_i[at]
+        slot = pick(lambda c, r: inv_t[r : r + 1, :], ROWS, hi, lo, [jnp.full((8, 128), -1, I32)])[0]
+        hi_i[at] = jnp.where(slot >= 0, slot >> 7, hi + FROWS)
+        lo_i[at] = jnp.where(slot >= 0, slot & 127, lo)
+        return carry
+
+    lax.fori_loop(0, 16, renumber, 0, unroll=4)
 
     def make_one_hot(i, carry):
-        oh[i] = one_hot(hi_i[pl.ds(i, 1), :], ROWS)
-        bt[:, pl.ds(pl.multiple_of(ELEM * i, ELEM), ELEM)] = one_hot(lo_i[pl.ds(i, 1), :], 128)
+        oh[i] = one_hot(hi_i[pl.ds(i, 1), :], FROWS + ROWS)
         return carry
 
     lax.fori_loop(0, NODES_PER, make_one_hot, 0)
+    turned = lo_i[...].astype(F32).T
+    number = lax.broadcasted_iota(I32, (ELEM, 128), 1).astype(F32)
+    for i in range(NODES_PER):
+        same = jnp.broadcast_to(turned[:, i : i + 1], (ELEM, 128)) == number
+        bn[ELEM * i : ELEM * i + ELEM, :] = jnp.where(same, 1.0, 0.0).astype(BF16)
+
+    for half in range(2):
+        hi, lo = f_hi[8 * half : 8 * half + 8, :], f_lo[8 * half : 8 * half + 8, :]
+        for source, target, idle in ((mi, mf, 1.0), (ri, rf, 0.0)):
+            got = pick(
+                lambda c, r: source[c * ROWS + r : c * ROWS + r + 1, :], ROWS, hi, lo,
+                [jnp.full((8, 128), idle, F32)] * 3,
+            )
+            for c in range(3):
+                target[c * FROWS + 8 * half : c * FROWS + 8 * half + 8, :] = got[c]
 
     row_of = lax.broadcasted_iota(I32, (96, 81), 0)
     col_of = lax.broadcasted_iota(I32, (96, 81), 1)
@@ -139,36 +183,22 @@
         p_hi[...] = high
         p_lo[...] = product - high
 
-    def scatter():
+    def scatter(first, rows):
         columns = []
         for i in range(NODES_PER):
-            hot = oh[i]
+            hot = oh[i, first : first + rows]
             blocks = []
             for part in (p_hi, p_lo):
                 for c in range(3):
                     row = part[c * 32 + i : c * 32 + i + 1, :]
-                    value = jnp.broadcast_to(row, (ROWS, ELEM)).astype(BF16)
+                    value = jnp.broadcast_to(row, (rows, ELEM)).astype(BF16)
                     blocks.append(value * hot)
             columns.append(jnp.concatenate(blocks, axis=0))
-        acc = dot(jnp.concatenate(columns, axis=1), bt[...], NT)
-        return acc[0:96] + acc[96:192]
-
-    acc = jnp.zeros((64, 128), F32)
-    for f in range(4):
-        face = face_ref[f : f + 1, :]
-        hot = one_hot(face >> 7, ROWS)
-        slot = lax.broadcasted_iota(I32, (ROWS, ELEM), 1) + (512 * f + 1)
-        a = jnp.concatenate(
-            [(slot >> 6).astype(F32).astype(BF16) * hot, (slot & 63).astype(F32).astype(BF16) * hot],
-            axis=0,
-        )
-        acc = acc + dot(a, one_hot(face & 127, 128), NT)
-    inverse = (64.0 * acc[0:32] + acc[32:64]).astype(I32) - 1
-    v_hi[...] = inverse >> 7
-    v_lo[...] = inverse & 127
+        acc = dot(jnp.concatenate(columns, axis=1), bn[...], NN)
+        return acc[0 : 3 * rows] + acc[3 * rows : 6 * rows]
 
     put_product(main_diag * coef)
-    w_t[...] = mass_t[...] + scatter()
+    wf[...] = mf[...] + scatter(0, FROWS)
 
     pl.semaphore_wait(barrier, n_dev + n_grp - 2)
 
@@ -176,13 +206,10 @@
     up_d, down_d = lax.rem(d + 1, n_dev), lax.rem(d + n_dev - 1, n_dev)
     partners = ((down_g, d), (up_g, d), (g, down_d), (g, up_d))
 
-    def exchange(k, cover=None):
-        for half in range(2):
-            hi, lo = f_hi[8 * half : 8 * half + 8, :], f_lo[8 * half : 8 * half + 8, :]
-            got = pick(lambda c, r: w_t[c * ROWS + r : c * ROWS + r + 1, :], ROWS, hi, lo, 3)
+    def send_faces(k):
+        for f in range(4):
             for c in range(3):
-                send[k, 2 * half, c] = got[c][0:4]
-                send[k, 2 * half + 1, c] = got[c][4:8]
+                send[k, f, c] = wf[c * FROWS + 4 * f : c * FROWS + 4 * f + 4, :]
         copies = []
         for f in range(4):
             copy = pltpu.make_async_remote_copy(
@@ -195,36 +222,58 @@
             )
             copy.start()
             copies.append(copy)
-        if cover is not None:
-            cover()
+        return copies
+
+    def add_faces(k, copies):
+        for copy in copies:
+            copy.wait()
         for f in range(4):
-            copies[f].wait()
-        for q in range(4):
-            hi, lo = v_hi[8 * q : 8 * q + 8, :], v_lo[8 * q : 8 * q + 8, :]
-            got = pick(
-                lambda c, r: recv[k, r // 4, c, r % 4 : r % 4 + 1, :], 16, hi, lo, 3
-            )
             for c in range(3):
-                at = slice(c * ROWS + 8 * q, c * ROWS + 8 * q + 8)
-                w_t[at, :] = w_t[at, :] + got[c]
-
-    def operate(k):
+                at = slice(c * FROWS + 4 * f, c * FROWS + 4 * f + 4)
+                wf[at, :] = wf[at, :] + recv[k, f, c]
+
+    def gather(table, first, rows, fresh):
         def body(v, carry):
             row = pl.multiple_of(8 * (v // 4), 8)
             lane = pl.multiple_of(128 * (v % 4), 128)
             hi, lo = hi_i[pl.ds(row, 8), pl.ds(lane, 128)], lo_i[pl.ds(row, 8), pl.ds(lane, 128)]
-            got = pick(lambda c, r: z_t[c * ROWS + r : c * ROWS + r + 1, :], ROWS, hi, lo, 3)
+            if fresh:
+                start = [jnp.zeros((8, 128), F32)] * 3
+            else:
+                start = [gath[pl.ds(row + 32 * c, 8), pl.ds(lane, 128)] for c in range(3)]
+            got = pick(
+                lambda c, r: table[c * rows + r : c * rows + r + 1, :], rows, hi - first, lo, start
+            )
             for c in range(3):
                 gath[pl.ds(row + 32 * c, 8), pl.ds(lane, 128)] = got[c]
             return carry
 
-        lax.fori_loop(0, 16, body, 0, unroll=4)
+        lax.fori_loop(0, 16, body, 0, unroll=8)
+
+    def gather_interior():
+        gather(zi, FROWS, ROWS, True)
+
+    def gather_faces():
+        gather(zf, 0, FROWS, False)
+
+    def operate(k, interior):
         gh, gl = split(gath[...])
         both = dot(m_hl[...], gh, NN)
         product = both[0:96] + both[96:192] + dot(m_hl[0:96, :], gl, NN)
         put_product(product * coef)
-        w_t[...] = mass_t[...] * z_t[...] + scatter()
-        exchange(k)
+        wf[...] = mf[...] * zf[...] + scatter(0, FROWS)
+        copies = send_faces(k)
+        wi[...] = mi[...] * zi[...] + scatter(FROWS, ROWS)
+        interior()
+        add_faces(k, copies)
+
+    def step_interior():
+        zi[...] = zi[...] + (ri[...] - wi[...]) * di[...]
+        gather_interior()
+
+    def step_faces():
+        zf[...] = zf[...] + (rf[...] - wf[...]) * df[...]
+        gather_faces()
 
     def make_interpolation():
         home = 6 * (n_dev * g + d)
@@ -245,18 +294,33 @@
 
         lax.fori_loop(0, 8, body, 0)
 
-    exchange(0, make_interpolation)
-    dinv_t[...] = DAMPING / w_t[...]
-    z_t[...] = rhs_t[...] * dinv_t[...]
-    operate(1)
-    z_t[...] = z_t[...] + (rhs_t[...] - w_t[...]) * dinv_t[...]
-    operate(2)
-
-    w_t[...] = rhs_t[...] - w_t[...]
+    copies = send_faces(0)
+    wi[...] = mi[...] + scatter(FROWS, ROWS)
+    di[...] = DAMPING / wi[...]
+    zi[...] = ri[...] * di[...]
+    gather_interior()
+    add_faces(0, copies)
+    df[...] = DAMPING / wf[...]
+    zf[...] = rf[...] * df[...]
+    gather_faces()
+    operate(1, step_interior)
+    step_faces()
+    operate(2, make_interpolation)
+
+    wf[...] = rf[...] - wf[...]
     flat[...] = jnp.zeros((8, 4096), F32)
+    for q in range(4):
+        hi, lo = v_hi[8 * q : 8 * q + 8, :], v_lo[8 * q : 8 * q + 8, :]
+        rows = [slice(c * ROWS + 8 * q, c * ROWS + 8 * q + 8) for c in range(3)]
+        got = pick(
+            lambda c, r: wf[c * FROWS + r : c * FROWS + r + 1, :], FROWS, hi, lo,
+            [ri[at, :] - wi[at, :] for at in rows],
+        )
+        for c in range(3):
+            wi[rows[c], :] = got[c]
     for c in range(3):
         for r in range(ROWS):
-            flat[c : c + 1, 128 * r : 128 * r + 128] = w_t[c * ROWS + r : c * ROWS + r + 1, :]
+            flat[c : c + 1, 128 * r : 128 * r + 128] = wi[c * ROWS + r : c * ROWS + r + 1, :]
     rh, rl = split(flat[0:8, :])
     left = jnp.concatenate([rh, rl], axis=0)
     first = dot(left, pwh[...], NT)
@@ -333,13 +397,36 @@
     flat[0:8, :] = first[0:8] + first[8:16] + dot(ch, pwl[...], NN)
     for c in range(3):
         for r in range(ROWS):
-            at = slice(c * ROWS + r, c * ROWS + r + 1)
-            z_t[at, :] = z_t[at, :] + flat[c : c + 1, 128 * r : 128 * r + 128]
-
-    operate(3)
-    z_t[...] = z_t[...] + (rhs_t[...] - w_t[...]) * dinv_t[...]
-    operate(4)
-    out_ref[...] = z_t[...] + (rhs_t[...] - w_t[...]) * dinv_t[...]
+            wi[c * ROWS + r : c * ROWS + r + 1, :] = flat[c : c + 1, 128 * r : 128 * r + 128]
+    zi[...] = zi[...] + wi[...]
+    for half in range(2):
+        hi, lo = f_hi[8 * half : 8 * half + 8, :], f_lo[8 * half : 8 * half + 8, :]
+        got = pick(
+            lambda c, r: wi[c * ROWS + r : c * ROWS + r + 1, :], ROWS, hi, lo,
+            [jnp.zeros((8, 128), F32)] * 3,
+        )
+        for c in range(3):
+            at = slice(c * FROWS + 8 * half, c * FROWS + 8 * half + 8)
+            zf[at, :] = zf[at, :] + got[c]
+    gather_interior()
+    gather_faces()
+    operate(3, step_interior)
+    step_faces()
+
+    def last_interior():
+        zi[...] = zi[...] + (ri[...] - wi[...]) * di[...]
+
+    operate(4, last_interior)
+    zf[...] = zf[...] + (rf[...] - wf[...]) * df[...]
+    for q in range(4):
+        hi, lo = v_hi[8 * q : 8 * q + 8, :], v_lo[8 * q : 8 * q + 8, :]
+        rows = [slice(c * ROWS + 8 * q, c * ROWS + 8 * q + 8) for c in range(3)]
+        got = pick(
+            lambda c, r: zf[c * FROWS + r : c * FROWS + r + 1, :], FROWS, hi, lo,
+            [zi[at, :] for at in rows],
+        )
+        for c in range(3):
+            out_ref[rows[c], :] = got[c]
 
 
 def solution(mesh):
@@ -358,21 +445,18 @@
             in_specs=[pl.BlockSpec(memory_space=pltpu.HBM)] * 9,
             out_specs=pl.BlockSpec(memory_space=pltpu.VMEM),
             scratch_shapes=[
-                pltpu.VMEM((96, 128), F32),
-                pltpu.VMEM((96, 128), F32),
-                pltpu.VMEM((96, 128), F32),
-                pltpu.VMEM((96, 128), F32),
-                pltpu.VMEM((96, 128), F32),
+                *[pltpu.VMEM((3 * n, 128), F32) for n in (FROWS, ROWS) * 5],
                 pltpu.VMEM((32, ELEM), I32),
                 pltpu.VMEM((32, ELEM), I32),
                 pltpu.VMEM((96, ELEM), F32),
                 pltpu.VMEM((96, ELEM), F32),
                 pltpu.VMEM((96, ELEM), F32),
                 pltpu.VMEM((192, 96), BF16),
-                pltpu.VMEM((128, NODES_PER * ELEM), BF16),
-                pltpu.VMEM((NODES_PER, ROWS, ELEM), BF16),
+                pltpu.VMEM((NODES_PER * ELEM, 128), BF16),
+                pltpu.VMEM((NODES_PER, FROWS + ROWS, ELEM), BF16),
                 pltpu.VMEM((16, 128), I32),
                 pltpu.VMEM((16, 128), I32),
+                pltpu.VMEM((32, 128), I32),
                 pltpu.VMEM((32, 128), I32),
                 pltpu.VMEM((32, 128), I32),
                 pltpu.VMEM((WIN, 4096), BF16),

time: 75.7 us -> 71.3 us (0.942)
  Pallas kernels: 73.9 us -> 69.5 us
    pallas_call x1, Pallas kernels: 73.9 us -> 69.5 us  [local(): pl.pallas_call(body, name='two_level', out_shape=jax.ShapeDtypeStruct((96...]
where the time goes in v3:
time: 71.3 us; the launch traced here: 71 us
  Pallas kernels  69.5 us (97%)
  local copies, waits for them, and re-layouts  1.42 us (2%)
    pallas_call x1, Pallas kernels, local(): pl.pallas_call(body, name='two_level', out_shape=jax.ShapeDtypeStruct((96...  69.5 us

profile of v3, /device:TPU:1, one launch (start us, length us, event | category | flops | bytes accessed | tf_op | source)
XLA Modules:
  0.0 71.0 jit_solution(2604684518416933610)
XLA Ops:
  0.0 69.5 %two_level.1 = f32[96,128]{1,0:T(8,128)} custom-call(f32[96,128]{1,0:T(8,128)} %bitcast.12, s32[27,4,128]{2,1,0:T(4,128)} %bitcast.11, f32[1,512]{1,0:T(1,128)} %bitcast.15, f32[96,128]{1,0:T(8,128)} %bitcast.13, s32[4,512]{1,0:T(4,128)} %bitcast.14, s32[4,4096]{1,0:T(4,128)} %bitcast.9, f32[4,4096]{1,0:T(4,128)} %bitcast.10, f32[81,81]{1,0:T(8,128)} %refs_7_.1, ...), custom_call_target="tpu_custom_call" | custom-call | tf_op jit(solution)/shard_map/two_level/pallas_call | solution.py:441
  69.6 1.4 %copy.13 = f32[1,1,3,4096]{3,1,2,0:T(1,128)} copy(f32[1,1,3,4096]{3,1,2,0:T(1,128)} %bitcast.8) | data formatting | bytes 98304

commit v4 on v3

--- a/solution.py
+++ b/solution.py
@@ -59,7 +59,7 @@
     out_ref,
     zf, zi, wf, wi, rf, ri, mf, mi, df, di,
     hi_i, lo_i, gath, p_hi, p_lo, m_hl, bn, oh,
-    f_hi, f_lo, v_hi, v_lo, inv_t, pwh, pwl, flat,
+    f_hi, f_lo, v_hi, v_lo, inv_t, pwh, pwl, pfh, pfl, lbh, lbl, win, flat,
     nodes_ref, coef_ref, face_ref, cn_ref, cw_ref, em_ref,
     send, recv, s1_send, s1_recv, s2_send, s2_recv, s3_send, s3_recv, lblk,
     send_sem, recv_sem, s1_ss, s1_rs, s2_ss, s2_rs, s3_ss, s3_rs, l_sem, in_sem,
@@ -145,37 +145,40 @@
 
     lax.fori_loop(0, 16, renumber, 0, unroll=4)
 
-    def make_one_hot(i, carry):
-        oh[i] = one_hot(hi_i[pl.ds(i, 1), :], FROWS + ROWS)
+    def one_hot_faces(i, carry):
+        oh[i, 0:FROWS] = one_hot(hi_i[pl.ds(i, 1), :], FROWS)
         return carry
 
-    lax.fori_loop(0, NODES_PER, make_one_hot, 0)
+    def one_hot_interior(i, carry):
+        oh[i, FROWS:] = one_hot(hi_i[pl.ds(i, 1), :] - FROWS, ROWS)
+        return carry
+
+    lax.fori_loop(0, NODES_PER, one_hot_faces, 0)
     turned = lo_i[...].astype(F32).T
     number = lax.broadcasted_iota(I32, (ELEM, 128), 1).astype(F32)
     for i in range(NODES_PER):
         same = jnp.broadcast_to(turned[:, i : i + 1], (ELEM, 128)) == number
         bn[ELEM * i : ELEM * i + ELEM, :] = jnp.where(same, 1.0, 0.0).astype(BF16)
 
-    for half in range(2):
-        hi, lo = f_hi[8 * half : 8 * half + 8, :], f_lo[8 * half : 8 * half + 8, :]
-        for source, target, idle in ((mi, mf, 1.0), (ri, rf, 0.0)):
+    def at_faces(source, target, idle):
+        for half in range(2):
+            hi, lo = f_hi[8 * half : 8 * half + 8, :], f_lo[8 * half : 8 * half + 8, :]
             got = pick(
                 lambda c, r: source[c * ROWS + r : c * ROWS + r + 1, :], ROWS, hi, lo,
                 [jnp.full((8, 128), idle, F32)] * 3,
             )
             for c in range(3):
                 target[c * FROWS + 8 * half : c * FROWS + 8 * half + 8, :] = got[c]
+
+    at_faces(mi, mf, 1.0)
 
     row_of = lax.broadcasted_iota(I32, (96, 81), 0)
     col_of = lax.broadcasted_iota(I32, (96, 81), 1)
     place = (col_of == 27 * (row_of // 32) + row_of % 32) & (row_of % 32 < 27)
     place = jnp.where(place, 1.0, 0.0)
-    matrix = dot_exact(dot_exact(place, em_ref[...], NN), place, NT)
-    mh, ml = split(matrix)
-    m_hl[0:96, :] = mh
-    m_hl[96:192, :] = ml
-    eye = lax.broadcasted_iota(I32, (96, 96), 0) == lax.broadcasted_iota(I32, (96, 96), 1)
-    main_diag = jnp.sum(jnp.where(eye, matrix, 0.0), axis=1, keepdims=True)
+    eye = lax.broadcasted_iota(I32, (81, 81), 0) == lax.broadcasted_iota(I32, (81, 81), 1)
+    diag_row = jnp.sum(jnp.where(eye, em_ref[...], 0.0), axis=0, keepdims=True)
+    main_diag = jnp.sum(place * diag_row, axis=1, keepdims=True)
     coef = coef_ref[...]
 
     def put_product(product):
@@ -232,7 +235,7 @@
                 at = slice(c * FROWS + 4 * f, c * FROWS + 4 * f + 4)
                 wf[at, :] = wf[at, :] + recv[k, f, c]
 
-    def gather(table, first, rows, fresh):
+    def gather(table, first, rows, fresh, unroll):
         def body(v, carry):
             row = pl.multiple_of(8 * (v // 4), 8)
             lane = pl.multiple_of(128 * (v % 4), 128)
@@ -248,13 +251,13 @@
                 gath[pl.ds(row + 32 * c, 8), pl.ds(lane, 128)] = got[c]
             return carry
 
-        lax.fori_loop(0, 16, body, 0, unroll=8)
+        lax.fori_loop(0, 16, body, 0, unroll=unroll)
 
     def gather_interior():
-        gather(zi, FROWS, ROWS, True)
+        gather(zi, FROWS, ROWS, True, 8)
 
     def gather_faces():
-        gather(zf, 0, FROWS, False)
+        gather(zf, 0, FROWS, False, 16)
 
     def operate(k, interior):
         gh, gl = split(gath[...])
@@ -275,56 +278,97 @@
         zf[...] = zf[...] + (rf[...] - wf[...]) * df[...]
         gather_faces()
 
+    home = 6 * (n_dev * g + d)
+
+    def fill(high_ref, low_ref, at, nodes, weights):
+        shape = (WIN, nodes[0].shape[1])
+        number = lax.broadcasted_iota(I32, shape, 0)
+        total = jnp.zeros(shape, F32)
+        for node, weight in zip(nodes, weights):
+            rel = node - home
+            rel = jnp.where(rel < 0, rel + CN, rel)
+            hit = jnp.broadcast_to(rel, shape) == number
+            total = total + jnp.where(hit, jnp.broadcast_to(weight, shape), 0.0)
+        high_ref[:, at], low_ref[:, at] = split(total)
+
     def make_interpolation():
-        home = 6 * (n_dev * g + d)
-
         def body(q, carry):
             at = pl.ds(pl.multiple_of(512 * q, 512), 512)
-            number = lax.broadcasted_iota(I32, (WIN, 512), 0)
-            total = jnp.zeros((WIN, 512), F32)
-            for j in range(4):
-                rel = cn_ref[j : j + 1, at] - home
-                rel = jnp.where(rel < 0, rel + CN, rel)
-                hit = jnp.broadcast_to(rel, (WIN, 512)) == number
-                total = total + jnp.where(hit, jnp.broadcast_to(cw_ref[j : j + 1, at], (WIN, 512)), 0.0)
-            high, low = split(total)
-            pwh[:, at] = high
-            pwl[:, at] = low
+            fill(
+                pwh, pwl, at,
+                [cn_ref[j : j + 1, at] for j in range(4)], [cw_ref[j : j + 1, at] for j in range(4)],
+            )
             return carry
 
         lax.fori_loop(0, 8, body, 0)
 
+    def make_face_interpolation():
+        for half in range(2):
+            hi, lo = f_hi[8 * half : 8 * half + 8, :], f_lo[8 * half : 8 * half + 8, :]
+            nodes = pick(
+                lambda c, r: cn_ref[c : c + 1, 128 * r : 128 * r + 128], ROWS, hi, lo,
+                [jnp.zeros((8, 128), I32)] * 4,
+            )
+            weights = pick(
+                lambda c, r: cw_ref[c : c + 1, 128 * r : 128 * r + 128], ROWS, hi, lo,
+                [jnp.zeros((8, 128), F32)] * 4,
+            )
+            for r in range(8):
+                at = slice(128 * (8 * half + r), 128 * (8 * half + r) + 128)
+                fill(
+                    pfh, pfl, at, [n[r : r + 1] for n in nodes], [w[r : r + 1] for w in weights]
+                )
+
+    def restricted(values, high_ref, low_ref):
+        rh, rl = split(values)
+        both = dot(jnp.concatenate([rh, rl], axis=0), high_ref[...], NT)
+        return both[0:8] + both[8:16] + dot(rh, low_ref[...], NT)
+
+    def residual_interior():
+        make_interpolation()
+        for b in range(6):
+            at = slice(128 * b, 128 * b + 128)
+            lbh[:, at], lbl[:, at] = split(lblk[b])
+        inside = v_hi[...] < 0
+        for c in range(3):
+            at = slice(c * ROWS, c * ROWS + ROWS)
+            wi[at, :] = jnp.where(inside, ri[at, :] - wi[at, :], 0.0)
+        flat[...] = jnp.zeros((8, 4096), F32)
+        for c in range(3):
+            for r in range(ROWS):
+                flat[c : c + 1, 128 * r : 128 * r + 128] = wi[c * ROWS + r : c * ROWS + r + 1, :]
+        win[...] = restricted(flat[...], pwh, pwl)
+
     copies = send_faces(0)
+    lax.fori_loop(0, NODES_PER, one_hot_interior, 0)
     wi[...] = mi[...] + scatter(FROWS, ROWS)
     di[...] = DAMPING / wi[...]
     zi[...] = ri[...] * di[...]
     gather_interior()
+    at_faces(ri, rf, 0.0)
+    mh, ml = split(dot_exact(dot_exact(place, em_ref[...], NN), place, NT))
+    m_hl[0:96, :] = mh
+    m_hl[96:192, :] = ml
     add_faces(0, copies)
     df[...] = DAMPING / wf[...]
     zf[...] = rf[...] * df[...]
     gather_faces()
-    operate(1, step_interior)
+    def first_interior():
+        step_interior()
+        make_face_interpolation()
+        for copy in l_copies:
+            copy.wait()
+
+    operate(1, first_interior)
     step_faces()
-    operate(2, make_interpolation)
+    operate(2, residual_interior)
 
     wf[...] = rf[...] - wf[...]
     flat[...] = jnp.zeros((8, 4096), F32)
-    for q in range(4):
-        hi, lo = v_hi[8 * q : 8 * q + 8, :], v_lo[8 * q : 8 * q + 8, :]
-        rows = [slice(c * ROWS + 8 * q, c * ROWS + 8 * q + 8) for c in range(3)]
-        got = pick(
-            lambda c, r: wf[c * FROWS + r : c * FROWS + r + 1, :], FROWS, hi, lo,
-            [ri[at, :] - wi[at, :] for at in rows],
-        )
-        for c in range(3):
-            wi[rows[c], :] = got[c]
     for c in range(3):
-        for r in range(ROWS):
-            flat[c : c + 1, 128 * r : 128 * r + 128] = wi[c * ROWS + r : c * ROWS + r + 1, :]
-    rh, rl = split(flat[0:8, :])
-    left = jnp.concatenate([rh, rl], axis=0)
-    first = dot(left, pwh[...], NT)
-    window = first[0:8] + first[8:16] + dot(rh, pwl[...], NT)
+        for r in range(FROWS):
+            flat[c : c + 1, 128 * r : 128 * r + 128] = wf[c * FROWS + r : c * FROWS + r + 1, :]
+    window = win[...] + restricted(flat[:, 0 : 128 * FROWS], pfh, pfl)
     for c in range(3):
         s1_send[:, WIN * c : WIN * c + WIN] = window[c : c + 1]
     s1_send[:, 3 * WIN :] = jnp.zeros((1, 256 - 3 * WIN), F32)
@@ -362,23 +406,24 @@
             values = lane_gather(windows[:, 128 * (c // 2) : 128 * (c // 2) + 128], at)
             row.append(jnp.sum(jnp.where(inside, values, 0.0), axis=0, keepdims=True))
         span.append(row)
-    for copy in l_copies:
-        copy.wait()
     acc = jnp.zeros((RB, 128), F32)
     for c in range(3):
         for b in range(2):
             acc = acc + lblk[2 * c + b] * span[c][b]
-    s2_send[...] = dot_exact(jnp.ones((8, 128), F32), acc, NT)[0:1]
+    ah, al = split(acc)
+    s2_send[...] = dot(jnp.ones((16, 256), BF16), jnp.concatenate([ah, al], axis=1), NT)[0:1]
     s2_recv[g] = s2_send[...]
     to_all(lambda peer: s2_send, s2_recv, s2_ss, s2_rs, False)
     halfway = jnp.sum(s2_recv[:, 0, :], axis=0, keepdims=True)
-    halfway = jnp.broadcast_to(halfway, (8, RB))
+    hh, hl = split(jnp.broadcast_to(halfway, (8, RB)))
+    both = dot(jnp.concatenate([hh, hl], axis=0), lbh[...], NN)
+    partial = both[0:1] + both[8:9] + dot(hh, lbl[...], NN)[0:1]
     parts = []
     for c in range(3):
         at = jnp.where(lane < WIN, lane, lane - WIN) + first_at
         values = []
         for b in range(2):
-            row = dot_exact(halfway, lblk[2 * c + b], NN)[0:1]
+            row = partial[:, 256 * c + 128 * b : 256 * c + 128 * b + 128]
             values.append(
                 lane_gather(jnp.broadcast_to(row, (n_dev, 128)), jnp.clip(at - 128 * b, 0, 127))
             )
@@ -393,21 +438,13 @@
     )
     ch, cl = split(correction)
     left = jnp.concatenate([ch, cl], axis=0)
-    first = dot(left, pwh[...], NN)
-    flat[0:8, :] = first[0:8] + first[8:16] + dot(ch, pwl[...], NN)
-    for c in range(3):
-        for r in range(ROWS):
-            wi[c * ROWS + r : c * ROWS + r + 1, :] = flat[c : c + 1, 128 * r : 128 * r + 128]
-    zi[...] = zi[...] + wi[...]
-    for half in range(2):
-        hi, lo = f_hi[8 * half : 8 * half + 8, :], f_lo[8 * half : 8 * half + 8, :]
-        got = pick(
-            lambda c, r: wi[c * ROWS + r : c * ROWS + r + 1, :], ROWS, hi, lo,
-            [jnp.zeros((8, 128), F32)] * 3,
-        )
+    for high, low, field, rows in ((pwh, pwl, zi, ROWS), (pfh, pfl, zf, FROWS)):
+        both = dot(left, high[...], NN)
+        flat[:, 0 : 128 * rows] = both[0:8] + both[8:16] + dot(ch, low[...], NN)
         for c in range(3):
-            at = slice(c * FROWS + 8 * half, c * FROWS + 8 * half + 8)
-            zf[at, :] = zf[at, :] + got[c]
+            for r in range(rows):
+                at = slice(c * rows + r, c * rows + r + 1)
+                field[at, :] = field[at, :] + flat[c : c + 1, 128 * r : 128 * r + 128]
     gather_interior()
     gather_faces()
     operate(3, step_interior)
@@ -461,6 +498,11 @@
                 pltpu.VMEM((32, 128), I32),
                 pltpu.VMEM((WIN, 4096), BF16),
                 pltpu.VMEM((WIN, 4096), BF16),
+                pltpu.VMEM((WIN, 128 * FROWS), BF16),
+                pltpu.VMEM((WIN, 128 * FROWS), BF16),
+                pltpu.VMEM((RB, 768), BF16),
+                pltpu.VMEM((RB, 768), BF16),
+                pltpu.VMEM((8, WIN), F32),
                 pltpu.VMEM((8, 4096), F32),
                 pltpu.VMEM((27, 4, 128), I32),
                 pltpu.VMEM((1, ELEM), F32),

time: 71.3 us -> 74 us (1.038)
  Pallas kernels: 69.5 us -> 72.3 us
    pallas_call x1, Pallas kernels: 69.5 us -> 72.3 us  [local(): pl.pallas_call(body, name='two_level', out_shape=jax.ShapeDtypeStruct((96...]
where the time goes in v4:
time: 74 us; the launch traced here: 73.7 us
  Pallas kernels  72.3 us (98%)
  local copies, waits for them, and re-layouts  1.42 us (2%)
    pallas_call x1, Pallas kernels, local(): pl.pallas_call(body, name='two_level', out_shape=jax.ShapeDtypeStruct((96...  72.3 us

profile of v4, /device:TPU:1, one launch (start us, length us, event | category | flops | bytes accessed | tf_op | source)
XLA Modules:
  0.0 73.7 jit_solution(4555801274400046051)
XLA Ops:
  0.0 72.3 %two_level.1 = f32[96,128]{1,0:T(8,128)} custom-call(f32[96,128]{1,0:T(8,128)} %bitcast.12, s32[27,4,128]{2,1,0:T(4,128)} %bitcast.11, f32[1,512]{1,0:T(1,128)} %bitcast.15, f32[96,128]{1,0:T(8,128)} %bitcast.13, s32[4,512]{1,0:T(4,128)} %bitcast.14, s32[4,4096]{1,0:T(4,128)} %bitcast.9, f32[4,4096]{1,0:T(4,128)} %bitcast.10, f32[81,81]{1,0:T(8,128)} %refs_7_.1, ...), custom_call_target="tpu_custom_call" | custom-call | tf_op jit(solution)/shard_map/two_level/pallas_call | solution.py:478
  72.3 1.4 %copy.13 = f32[1,1,3,4096]{3,1,2,0:T(1,128)} copy(f32[1,1,3,4096]{3,1,2,0:T(1,128)} %bitcast.8) | data formatting | bytes 98304

commit v5 on v4

--- a/solution.py
+++ b/solution.py
@@ -59,7 +59,7 @@
     out_ref,
     zf, zi, wf, wi, rf, ri, mf, mi, df, di,
     hi_i, lo_i, gath, p_hi, p_lo, m_hl, bn, oh,
-    f_hi, f_lo, v_hi, v_lo, inv_t, pwh, pwl, pfh, pfl, lbh, lbl, win, flat,
+    f_hi, f_lo, v_hi, v_lo, inv_t, pwh, pwl, lbh, lbl, flat,
     nodes_ref, coef_ref, face_ref, cn_ref, cw_ref, em_ref,
     send, recv, s1_send, s1_recv, s2_send, s2_recv, s3_send, s3_recv, lblk,
     send_sem, recv_sem, s1_ss, s1_rs, s2_ss, s2_rs, s3_ss, s3_rs, l_sem, in_sem,
@@ -200,11 +200,6 @@
         acc = dot(jnp.concatenate(columns, axis=1), bn[...], NN)
         return acc[0 : 3 * rows] + acc[3 * rows : 6 * rows]
 
-    put_product(main_diag * coef)
-    wf[...] = mf[...] + scatter(0, FROWS)
-
-    pl.semaphore_wait(barrier, n_dev + n_grp - 2)
-
     up_g, down_g = lax.rem(g + 1, n_grp), lax.rem(g + n_grp - 1, n_grp)
     up_d, down_d = lax.rem(d + 1, n_dev), lax.rem(d + n_dev - 1, n_dev)
     partners = ((down_g, d), (up_g, d), (g, down_d), (g, up_d))
@@ -257,26 +252,7 @@
         gather(zi, FROWS, ROWS, True, 8)
 
     def gather_faces():
-        gather(zf, 0, FROWS, False, 16)
-
-    def operate(k, interior):
-        gh, gl = split(gath[...])
-        both = dot(m_hl[...], gh, NN)
-        product = both[0:96] + both[96:192] + dot(m_hl[0:96, :], gl, NN)
-        put_product(product * coef)
-        wf[...] = mf[...] * zf[...] + scatter(0, FROWS)
-        copies = send_faces(k)
-        wi[...] = mi[...] * zi[...] + scatter(FROWS, ROWS)
-        interior()
-        add_faces(k, copies)
-
-    def step_interior():
-        zi[...] = zi[...] + (ri[...] - wi[...]) * di[...]
-        gather_interior()
-
-    def step_faces():
-        zf[...] = zf[...] + (rf[...] - wf[...]) * df[...]
-        gather_faces()
+        gather(zf, 0, FROWS, False, 8)
 
     home = 6 * (n_dev * g + d)
 
@@ -302,159 +278,194 @@
 
         lax.fori_loop(0, 8, body, 0)
 
-    def make_face_interpolation():
-        for half in range(2):
-            hi, lo = f_hi[8 * half : 8 * half + 8, :], f_lo[8 * half : 8 * half + 8, :]
-            nodes = pick(
-                lambda c, r: cn_ref[c : c + 1, 128 * r : 128 * r + 128], ROWS, hi, lo,
-                [jnp.zeros((8, 128), I32)] * 4,
-            )
-            weights = pick(
-                lambda c, r: cw_ref[c : c + 1, 128 * r : 128 * r + 128], ROWS, hi, lo,
-                [jnp.zeros((8, 128), F32)] * 4,
-            )
-            for r in range(8):
-                at = slice(128 * (8 * half + r), 128 * (8 * half + r) + 128)
-                fill(
-                    pfh, pfl, at, [n[r : r + 1] for n in nodes], [w[r : r + 1] for w in weights]
-                )
-
     def restricted(values, high_ref, low_ref):
         rh, rl = split(values)
         both = dot(jnp.concatenate([rh, rl], axis=0), high_ref[...], NT)
         return both[0:8] + both[8:16] + dot(rh, low_ref[...], NT)
 
-    def residual_interior():
-        make_interpolation()
-        for b in range(6):
-            at = slice(128 * b, 128 * b + 128)
-            lbh[:, at], lbl[:, at] = split(lblk[b])
-        inside = v_hi[...] < 0
-        for c in range(3):
-            at = slice(c * ROWS, c * ROWS + ROWS)
-            wi[at, :] = jnp.where(inside, ri[at, :] - wi[at, :], 0.0)
-        flat[...] = jnp.zeros((8, 4096), F32)
+    def coarse_correction():
+        for q in range(4):
+            hi, lo = v_hi[8 * q : 8 * q + 8, :], v_lo[8 * q : 8 * q + 8, :]
+            rows = [slice(c * ROWS + 8 * q, c * ROWS + 8 * q + 8) for c in range(3)]
+            got = pick(
+                lambda c, r: wf[c * FROWS + r : c * FROWS + r + 1, :], FROWS, hi, lo,
+                [wi[at, :] for at in rows],
+            )
+            for c in range(3):
+                wi[rows[c], :] = got[c]
         for c in range(3):
             for r in range(ROWS):
                 flat[c : c + 1, 128 * r : 128 * r + 128] = wi[c * ROWS + r : c * ROWS + r + 1, :]
-        win[...] = restricted(flat[...], pwh, pwl)
-
-    copies = send_faces(0)
-    lax.fori_loop(0, NODES_PER, one_hot_interior, 0)
-    wi[...] = mi[...] + scatter(FROWS, ROWS)
-    di[...] = DAMPING / wi[...]
-    zi[...] = ri[...] * di[...]
-    gather_interior()
-    at_faces(ri, rf, 0.0)
-    mh, ml = split(dot_exact(dot_exact(place, em_ref[...], NN), place, NT))
-    m_hl[0:96, :] = mh
-    m_hl[96:192, :] = ml
-    add_faces(0, copies)
-    df[...] = DAMPING / wf[...]
-    zf[...] = rf[...] * df[...]
-    gather_faces()
-    def first_interior():
-        step_interior()
-        make_face_interpolation()
-        for copy in l_copies:
-            copy.wait()
-
-    operate(1, first_interior)
-    step_faces()
-    operate(2, residual_interior)
-
-    wf[...] = rf[...] - wf[...]
-    flat[...] = jnp.zeros((8, 4096), F32)
-    for c in range(3):
-        for r in range(FROWS):
-            flat[c : c + 1, 128 * r : 128 * r + 128] = wf[c * FROWS + r : c * FROWS + r + 1, :]
-    window = win[...] + restricted(flat[:, 0 : 128 * FROWS], pfh, pfl)
-    for c in range(3):
-        s1_send[:, WIN * c : WIN * c + WIN] = window[c : c + 1]
-    s1_send[:, 3 * WIN :] = jnp.zeros((1, 256 - 3 * WIN), F32)
-    s1_recv[d] = s1_send[...]
-    lane = lax.broadcasted_iota(I32, (n_dev, 128), 1)
-    first_at = 6 * lax.broadcasted_iota(I32, (n_dev, 128), 0) + (96 * g - 128 * block0)
-
-    def to_all(src, dst, send_sems, recv_sems, along_dev):
-        me, count = (d, n_dev) if along_dev else (g, n_grp)
-        copies = []
-        for k in range(1, count):
-            peer = lax.rem(me + k, count)
-            copy = pltpu.make_async_remote_copy(
-                src_ref=src(peer),
-                dst_ref=dst.at[me],
-                send_sem=send_sems.at[k],
-                recv_sem=recv_sems.at[k],
-                device_id=(g, peer) if along_dev else (peer, d),
-                device_id_type=MESH,
-            )
-            copy.start()
-            copies.append(copy)
-        for copy in copies:
-            copy.wait()
-
-    to_all(lambda peer: s1_send, s1_recv, s1_ss, s1_rs, True)
-    windows = s1_recv[:, 0, :]
-    span = []
-    for c in range(3):
-        row = []
-        for b in range(2):
-            at = lane + 128 * b - first_at
-            inside = (at >= 0) & (at < WIN)
-            at = jnp.where(inside, at, 0) + WIN * (c % 2)
-            values = lane_gather(windows[:, 128 * (c // 2) : 128 * (c // 2) + 128], at)
-            row.append(jnp.sum(jnp.where(inside, values, 0.0), axis=0, keepdims=True))
-        span.append(row)
-    acc = jnp.zeros((RB, 128), F32)
-    for c in range(3):
-        for b in range(2):
-            acc = acc + lblk[2 * c + b] * span[c][b]
-    ah, al = split(acc)
-    s2_send[...] = dot(jnp.ones((16, 256), BF16), jnp.concatenate([ah, al], axis=1), NT)[0:1]
-    s2_recv[g] = s2_send[...]
-    to_all(lambda peer: s2_send, s2_recv, s2_ss, s2_rs, False)
-    halfway = jnp.sum(s2_recv[:, 0, :], axis=0, keepdims=True)
-    hh, hl = split(jnp.broadcast_to(halfway, (8, RB)))
-    both = dot(jnp.concatenate([hh, hl], axis=0), lbh[...], NN)
-    partial = both[0:1] + both[8:9] + dot(hh, lbl[...], NN)[0:1]
-    parts = []
-    for c in range(3):
-        at = jnp.where(lane < WIN, lane, lane - WIN) + first_at
-        values = []
-        for b in range(2):
-            row = partial[:, 256 * c + 128 * b : 256 * c + 128 * b + 128]
-            values.append(
-                lane_gather(jnp.broadcast_to(row, (n_dev, 128)), jnp.clip(at - 128 * b, 0, 127))
-            )
-        parts.append(jnp.where(at < 128, values[0], values[1]))
-    s3_send[:, 0, 0:128] = jnp.where(lane < WIN, parts[0], parts[1])
-    s3_send[:, 0, 128:256] = parts[2]
-    s3_recv[d] = s3_send[d]
-    to_all(lambda peer: s3_send.at[peer], s3_recv, s3_ss, s3_rs, True)
-    total = jnp.sum(s3_recv[:, 0, :], axis=0, keepdims=True)
-    correction = jnp.concatenate(
-        [total[:, WIN * c : WIN * c + WIN] for c in range(3)] + [jnp.zeros((5, WIN), F32)], axis=0
-    )
-    ch, cl = split(correction)
-    left = jnp.concatenate([ch, cl], axis=0)
-    for high, low, field, rows in ((pwh, pwl, zi, ROWS), (pfh, pfl, zf, FROWS)):
-        both = dot(left, high[...], NN)
-        flat[:, 0 : 128 * rows] = both[0:8] + both[8:16] + dot(ch, low[...], NN)
-        for c in range(3):
-            for r in range(rows):
-                at = slice(c * rows + r, c * rows + r + 1)
-                field[at, :] = field[at, :] + flat[c : c + 1, 128 * r : 128 * r + 128]
-    gather_interior()
-    gather_faces()
-    operate(3, step_interior)
-    step_faces()
-
-    def last_interior():
-        zi[...] = zi[...] + (ri[...] - wi[...]) * di[...]
-
-    operate(4, last_interior)
-    zf[...] = zf[...] + (rf[...] - wf[...]) * df[...]
+        window = restricted(flat[...], pwh, pwl)
+        for c in range(3):
+            s1_send[:, WIN * c : WIN * c + WIN] = window[c : c + 1]
+        s1_send[:, 3 * WIN :] = jnp.zeros((1, 256 - 3 * WIN), F32)
+        s1_recv[d] = s1_send[...]
+        lane = lax.broadcasted_iota(I32, (n_dev, 128), 1)
+        first_at = 6 * lax.broadcasted_iota(I32, (n_dev, 128), 0) + (96 * g - 128 * block0)
+
+        def to_all(src, dst, send_sems, recv_sems, along_dev, cover=None):
+            me, count = (d, n_dev) if along_dev else (g, n_grp)
+            copies = []
+            for k in range(1, count):
+                peer = lax.rem(me + k, count)
+                copy = pltpu.make_async_remote_copy(
+                    src_ref=src(peer),
+                    dst_ref=dst.at[me],
+                    send_sem=send_sems.at[k],
+                    recv_sem=recv_sems.at[k],
+                    device_id=(g, peer) if along_dev else (peer, d),
+                    device_id_type=MESH,
+                )
+                copy.start()
+                copies.append(copy)
+            if cover is not None:
+                cover()
+            for copy in copies:
+                copy.wait()
+
+        def split_factor():
+            for copy in l_copies:
+                copy.wait()
+            for b in range(6):
+                at = slice(128 * b, 128 * b + 128)
+                lbh[:, at], lbl[:, at] = split(lblk[b])
+
+        to_all(lambda peer: s1_send, s1_recv, s1_ss, s1_rs, True, split_factor)
+        windows = s1_recv[:, 0, :]
+        span = []
+        for c in range(3):
+            row = []
+            for b in range(2):
+                at = lane + 128 * b - first_at
+                inside = (at >= 0) & (at < WIN)
+                at = jnp.where(inside, at, 0) + WIN * (c % 2)
+                values = lane_gather(windows[:, 128 * (c // 2) : 128 * (c // 2) + 128], at)
+                row.append(jnp.sum(jnp.where(inside, values, 0.0), axis=0, keepdims=True))
+            span.append(row)
+        acc = jnp.zeros((RB, 128), F32)
+        for c in range(3):
+            for b in range(2):
+                acc = acc + lblk[2 * c + b] * span[c][b]
+        ah, al = split(acc)
+        s2_send[...] = dot(jnp.ones((16, 256), BF16), jnp.concatenate([ah, al], axis=1), NT)[0:1]
+        s2_recv[g] = s2_send[...]
+        to_all(lambda peer: s2_send, s2_recv, s2_ss, s2_rs, False)
+        halfway = jnp.sum(s2_recv[:, 0, :], axis=0, keepdims=True)
+        hh, hl = split(jnp.broadcast_to(halfway, (8, RB)))
+        both = dot(jnp.concatenate([hh, hl], axis=0), lbh[...], NN)
+        partial = both[0:1] + both[8:9] + dot(hh, lbl[...], NN)[0:1]
+        parts = []
+        for c in range(3):
+            at = jnp.where(lane < WIN, lane, lane - WIN) + first_at
+            values = []
+            for b in range(2):
+                row = partial[:, 256 * c + 128 * b : 256 * c + 128 * b + 128]
+                values.append(
+                    lane_gather(jnp.broadcast_to(row, (n_dev, 128)), jnp.clip(at - 128 * b, 0, 127))
+                )
+            parts.append(jnp.where(at < 128, values[0], values[1]))
+        s3_send[:, 0, 0:128] = jnp.where(lane < WIN, parts[0], parts[1])
+        s3_send[:, 0, 128:256] = parts[2]
+        s3_recv[d] = s3_send[d]
+        to_all(lambda peer: s3_send.at[peer], s3_recv, s3_ss, s3_rs, True)
+        total = jnp.sum(s3_recv[:, 0, :], axis=0, keepdims=True)
+        correction = jnp.concatenate(
+            [total[:, WIN * c : WIN * c + WIN] for c in range(3)] + [jnp.zeros((5, WIN), F32)], axis=0
+        )
+        ch, cl = split(correction)
+        left = jnp.concatenate([ch, cl], axis=0)
+        both = dot(left, pwh[...], NN)
+        flat[...] = both[0:8] + both[8:16] + dot(ch, pwl[...], NN)
+        for c in range(3):
+            for r in range(ROWS):
+                wi[c * ROWS + r : c * ROWS + r + 1, :] = flat[c : c + 1, 128 * r : 128 * r + 128]
+        zi[...] = zi[...] + wi[...]
+        for half in range(2):
+            hi, lo = f_hi[8 * half : 8 * half + 8, :], f_lo[8 * half : 8 * half + 8, :]
+            got = pick(
+                lambda c, r: wi[c * ROWS + r : c * ROWS + r + 1, :], ROWS, hi, lo,
+                [jnp.zeros((8, 128), F32)] * 3,
+            )
+            for c in range(3):
+                at = slice(c * FROWS + 8 * half, c * FROWS + 8 * half + 8)
+                zf[at, :] = zf[at, :] + got[c]
+        gather_interior()
+
+    def apply(k, carry):
+        @pl.when(k == 0)
+        def _():
+            put_product(main_diag * coef)
+
+        @pl.when(k > 0)
+        def _():
+            gh, gl = split(gath[...])
+            both = dot(m_hl[...], gh, NN)
+            product = both[0:96] + both[96:192] + dot(m_hl[0:96, :], gl, NN)
+            put_product(product * coef)
+
+        wf[...] = mf[...] * zf[...] + scatter(0, FROWS)
+
+        @pl.when(k == 0)
+        def _():
+            pl.semaphore_wait(barrier, n_dev + n_grp - 2)
+
+        copies = send_faces(k)
+
+        @pl.when(k == 0)
+        def _():
+            lax.fori_loop(0, NODES_PER, one_hot_interior, 0)
+
+        wi[...] = mi[...] * zi[...] + scatter(FROWS, ROWS)
+
+        @pl.when(k == 0)
+        def _():
+            di[...] = DAMPING / wi[...]
+            zi[...] = ri[...] * di[...]
+            at_faces(ri, rf, 0.0)
+            mh, ml = split(dot_exact(dot_exact(place, em_ref[...], NN), place, NT))
+            m_hl[0:96, :] = mh
+            m_hl[96:192, :] = ml
+
+        @pl.when(k == 2)
+        def _():
+            wi[...] = ri[...] - wi[...]
+            flat[...] = jnp.zeros((8, 4096), F32)
+            make_interpolation()
+
+        @pl.when((k != 0) & (k != 2))
+        def _():
+            zi[...] = zi[...] + (ri[...] - wi[...]) * di[...]
+
+        @pl.when((k != 2) & (k != 4))
+        def _():
+            gather_interior()
+
+        add_faces(k, copies)
+
+        @pl.when(k == 0)
+        def _():
+            df[...] = DAMPING / wf[...]
+            zf[...] = rf[...] * df[...]
+
+        @pl.when(k == 2)
+        def _():
+            wf[...] = rf[...] - wf[...]
+            coarse_correction()
+
+        @pl.when((k != 0) & (k != 2))
+        def _():
+            zf[...] = zf[...] + (rf[...] - wf[...]) * df[...]
+
+        @pl.when(k != 4)
+        def _():
+            gather_faces()
+
+        return carry
+
+    zf[...] = jnp.ones((3 * FROWS, 128), F32)
+    zi[...] = jnp.ones((3 * ROWS, 128), F32)
+    lax.fori_loop(0, 5, apply, 0)
     for q in range(4):
         hi, lo = v_hi[8 * q : 8 * q + 8, :], v_lo[8 * q : 8 * q + 8, :]
         rows = [slice(c * ROWS + 8 * q, c * ROWS + 8 * q + 8) for c in range(3)]
@@ -498,11 +509,8 @@
                 pltpu.VMEM((32, 128), I32),
                 pltpu.VMEM((WIN, 4096), BF16),
                 pltpu.VMEM((WIN, 4096), BF16),
-                pltpu.VMEM((WIN, 128 * FROWS), BF16),
-                pltpu.VMEM((WIN, 128 * FROWS), BF16),
                 pltpu.VMEM((RB, 768), BF16),
                 pltpu.VMEM((RB, 768), BF16),
-                pltpu.VMEM((8, WIN), F32),
                 pltpu.VMEM((8, 4096), F32),
                 pltpu.VMEM((27, 4, 128), I32),
                 pltpu.VMEM((1, ELEM), F32),

time: 74 us -> 71 us (0.959)
  Pallas kernels: 72.3 us -> 69.2 us
    pallas_call x1, Pallas kernels: 72.3 us -> 69.2 us  [local(): pl.pallas_call(body, name='two_level', out_shape=jax.ShapeDtypeStruct((96...]
where the time goes in v5:
time: 71 us; the launch traced here: 70.6 us
  Pallas kernels  69.2 us (97%)
  local copies, waits for them, and re-layouts  1.42 us (2%)
    pallas_call x1, Pallas kernels, local(): pl.pallas_call(body, name='two_level', out_shape=jax.ShapeDtypeStruct((96...  69.2 us
    unnamed x1, local copies, waits for them, and re-layouts  1.42 us

profile of v5, /device:TPU:1, one launch (start us, length us, event | category | flops | bytes accessed | tf_op | source)
XLA Modules:
  0.0 70.6 jit_solution(7430534574401273541)
XLA Ops:
  0.0 69.2 %two_level.1 = f32[96,128]{1,0:T(8,128)} custom-call(f32[96,128]{1,0:T(8,128)} %bitcast.12, s32[27,4,128]{2,1,0:T(4,128)} %bitcast.11, f32[1,512]{1,0:T(1,128)} %bitcast.15, f32[96,128]{1,0:T(8,128)} %bitcast.13, s32[4,512]{1,0:T(4,128)} %bitcast.14, s32[4,4096]{1,0:T(4,128)} %bitcast.9, f32[4,4096]{1,0:T(4,128)} %bitcast.10, f32[81,81]{1,0:T(8,128)} %refs_7_.1, ...), custom_call_target="tpu_custom_call" | custom-call | tf_op jit(solution)/shard_map/two_level/pallas_call | solution.py:489
  69.2 1.4 %copy.13 = f32[1,1,3,4096]{3,1,2,0:T(1,128)} copy(f32[1,1,3,4096]{3,1,2,0:T(1,128)} %bitcast.8) | data formatting | bytes 98304

commit v6 on v5

--- a/solution.py
+++ b/solution.py
@@ -58,7 +58,7 @@
     rhs_hbm, nodes_hbm, coef_hbm, mass_hbm, face_hbm, cn_hbm, cw_hbm, em_hbm, chol_ref,
     out_ref,
     zf, zi, wf, wi, rf, ri, mf, mi, df, di,
-    hi_i, lo_i, gath, p_hi, p_lo, m_hl, bn, oh,
+    hi_i, lo_i, gath, p_hi, p_lo, m_hl, bn, hot_g, hot_d, oh,
     f_hi, f_lo, v_hi, v_lo, inv_t, pwh, pwl, lbh, lbl, flat,
     nodes_ref, coef_ref, face_ref, cn_ref, cw_ref, em_ref,
     send, recv, s1_send, s1_recv, s2_send, s2_recv, s3_send, s3_recv, lblk,
@@ -145,12 +145,16 @@
 
     lax.fori_loop(0, 16, renumber, 0, unroll=4)
 
+    twice = lax.broadcasted_iota(I32, (16, ELEM), 0) % 8
+
     def one_hot_faces(i, carry):
-        oh[i, 0:FROWS] = one_hot(hi_i[pl.ds(i, 1), :], FROWS)
+        at = jnp.broadcast_to(hi_i[pl.ds(i, 1), :], (16, ELEM))
+        hot_g[i] = jnp.where(at == twice, 1.0, 0.0).astype(BF16)
+        hot_d[i] = jnp.where(at == twice + 8, 1.0, 0.0).astype(BF16)
         return carry
 
     def one_hot_interior(i, carry):
-        oh[i, FROWS:] = one_hot(hi_i[pl.ds(i, 1), :] - FROWS, ROWS)
+        oh[i] = one_hot(hi_i[pl.ds(i, 1), :] - FROWS, ROWS)
         return carry
 
     lax.fori_loop(0, NODES_PER, one_hot_faces, 0)
@@ -186,10 +190,10 @@
         p_hi[...] = high
         p_lo[...] = product - high
 
-    def scatter(first, rows):
+    def scatter(rows):
         columns = []
         for i in range(NODES_PER):
-            hot = oh[i, first : first + rows]
+            hot = oh[i]
             blocks = []
             for part in (p_hi, p_lo):
                 for c in range(3):
@@ -200,16 +204,32 @@
         acc = dot(jnp.concatenate(columns, axis=1), bn[...], NN)
         return acc[0 : 3 * rows] + acc[3 * rows : 6 * rows]
 
+    def scatter_faces(hots):
+        columns = []
+        for i in range(NODES_PER):
+            hot = hots[i]
+            blocks = []
+            for c in range(3):
+                at = slice(c * 32 + i, c * 32 + i + 1)
+                value = jnp.concatenate(
+                    [jnp.broadcast_to(p_hi[at, :], (8, ELEM)), jnp.broadcast_to(p_lo[at, :], (8, ELEM))],
+                    axis=0,
+                )
+                blocks.append(value.astype(BF16) * hot)
+            columns.append(jnp.concatenate(blocks, axis=0))
+        acc = dot(jnp.concatenate(columns, axis=1), bn[...], NN)
+        return [acc[16 * c : 16 * c + 8] + acc[16 * c + 8 : 16 * c + 16] for c in range(3)]
+
     up_g, down_g = lax.rem(g + 1, n_grp), lax.rem(g + n_grp - 1, n_grp)
     up_d, down_d = lax.rem(d + 1, n_dev), lax.rem(d + n_dev - 1, n_dev)
     partners = ((down_g, d), (up_g, d), (g, down_d), (g, up_d))
 
-    def send_faces(k):
-        for f in range(4):
+    def send_faces(k, faces):
+        for f in faces:
             for c in range(3):
                 send[k, f, c] = wf[c * FROWS + 4 * f : c * FROWS + 4 * f + 4, :]
         copies = []
-        for f in range(4):
+        for f in faces:
             copy = pltpu.make_async_remote_copy(
                 src_ref=send.at[k, f],
                 dst_ref=recv.at[k, f ^ 1],
@@ -222,15 +242,15 @@
             copies.append(copy)
         return copies
 
-    def add_faces(k, copies):
+    def add_faces(k, faces, copies):
         for copy in copies:
             copy.wait()
-        for f in range(4):
+        for f in faces:
             for c in range(3):
                 at = slice(c * FROWS + 4 * f, c * FROWS + 4 * f + 4)
                 wf[at, :] = wf[at, :] + recv[k, f, c]
 
-    def gather(table, first, rows, fresh, unroll):
+    def gather(table, stride, base, first, rows, fresh, unroll):
         def body(v, carry):
             row = pl.multiple_of(8 * (v // 4), 8)
             lane = pl.multiple_of(128 * (v % 4), 128)
@@ -240,7 +260,8 @@
             else:
                 start = [gath[pl.ds(row + 32 * c, 8), pl.ds(lane, 128)] for c in range(3)]
             got = pick(
-                lambda c, r: table[c * rows + r : c * rows + r + 1, :], rows, hi - first, lo, start
+                lambda c, r: table[c * stride + base + r : c * stride + base + r + 1, :],
+                rows, hi - first, lo, start,
             )
             for c in range(3):
                 gath[pl.ds(row + 32 * c, 8), pl.ds(lane, 128)] = got[c]
@@ -249,10 +270,25 @@
         lax.fori_loop(0, 16, body, 0, unroll=unroll)
 
     def gather_interior():
-        gather(zi, FROWS, ROWS, True, 8)
-
-    def gather_faces():
-        gather(zf, 0, FROWS, False, 8)
+        gather(zi, ROWS, 0, FROWS, ROWS, True, 8)
+
+    def gather_faces(base):
+        gather(zf, FROWS, base, base, 8, False, 8)
+
+    def face_rows(base):
+        return [slice(c * FROWS + base, c * FROWS + base + 8) for c in range(3)]
+
+    def step_faces(k, base):
+        @pl.when(k == 0)
+        def _():
+            for at in face_rows(base):
+                df[at, :] = DAMPING / wf[at, :]
+                zf[at, :] = rf[at, :] * df[at, :]
+
+        @pl.when((k != 0) & (k != 2))
+        def _():
+            for at in face_rows(base):
+                zf[at, :] = zf[at, :] + (rf[at, :] - wf[at, :]) * df[at, :]
 
     home = 6 * (n_dev * g + d)
 
@@ -391,6 +427,7 @@
                 at = slice(c * FROWS + 8 * half, c * FROWS + 8 * half + 8)
                 zf[at, :] = zf[at, :] + got[c]
         gather_interior()
+        gather_faces(0)
 
     def apply(k, carry):
         @pl.when(k == 0)
@@ -404,19 +441,23 @@
             product = both[0:96] + both[96:192] + dot(m_hl[0:96, :], gl, NN)
             put_product(product * coef)
 
-        wf[...] = mf[...] * zf[...] + scatter(0, FROWS)
+        for at, part in zip(face_rows(8), scatter_faces(hot_d)):
+            wf[at, :] = mf[at, :] * zf[at, :] + part
 
         @pl.when(k == 0)
         def _():
             pl.semaphore_wait(barrier, n_dev + n_grp - 2)
 
-        copies = send_faces(k)
+        far = send_faces(k, (2, 3))
+        for at, part in zip(face_rows(0), scatter_faces(hot_g)):
+            wf[at, :] = mf[at, :] * zf[at, :] + part
+        near = send_faces(k, (0, 1))
 
         @pl.when(k == 0)
         def _():
             lax.fori_loop(0, NODES_PER, one_hot_interior, 0)
 
-        wi[...] = mi[...] * zi[...] + scatter(FROWS, ROWS)
+        wi[...] = mi[...] * zi[...] + scatter(ROWS)
 
         @pl.when(k == 0)
         def _():
@@ -441,25 +482,24 @@
         def _():
             gather_interior()
 
-        add_faces(k, copies)
-
-        @pl.when(k == 0)
-        def _():
-            df[...] = DAMPING / wf[...]
-            zf[...] = rf[...] * df[...]
+        add_faces(k, (0, 1), near)
+        step_faces(k, 0)
+
+        @pl.when((k != 2) & (k != 4))
+        def _():
+            gather_faces(0)
+
+        add_faces(k, (2, 3), far)
+        step_faces(k, 8)
 
         @pl.when(k == 2)
         def _():
             wf[...] = rf[...] - wf[...]
             coarse_correction()
 
-        @pl.when((k != 0) & (k != 2))
-        def _():
-            zf[...] = zf[...] + (rf[...] - wf[...]) * df[...]
-
         @pl.when(k != 4)
         def _():
-            gather_faces()
+            gather_faces(8)
 
         return carry
 
@@ -501,7 +541,9 @@
                 pltpu.VMEM((96, ELEM), F32),
                 pltpu.VMEM((192, 96), BF16),
                 pltpu.VMEM((NODES_PER * ELEM, 128), BF16),
-                pltpu.VMEM((NODES_PER, FROWS + ROWS, ELEM), BF16),
+                pltpu.VMEM((NODES_PER, 16, ELEM), BF16),
+                pltpu.VMEM((NODES_PER, 16, ELEM), BF16),
+                pltpu.VMEM((NODES_PER, ROWS, ELEM), BF16),
                 pltpu.VMEM((16, 128), I32),
                 pltpu.VMEM((16, 128), I32),
                 pltpu.VMEM((32, 128), I32),

time: 71 us -> 73 us (1.028)
  Pallas kernels: 69.2 us -> 71.5 us
    pallas_call x1, Pallas kernels: 69.2 us -> 71.5 us  [local(): pl.pallas_call(body, name='two_level', out_shape=jax.ShapeDtypeStruct((96...]
where the time goes in v6:
time: 73 us; the launch traced here: 72.9 us
  Pallas kernels  71.5 us (98%)
  local copies, waits for them, and re-layouts  1.42 us (2%)
    pallas_call x1, Pallas kernels, local(): pl.pallas_call(body, name='two_level', out_shape=jax.ShapeDtypeStruct((96...  71.5 us

profile of v6, /device:TPU:1, one launch (start us, length us, event | category | flops | bytes accessed | tf_op | source)
XLA Modules:
  0.0 72.9 jit_solution(6068247372989765483)
XLA Ops:
  0.0 71.5 %two_level.1 = f32[96,128]{1,0:T(8,128)} custom-call(f32[96,128]{1,0:T(8,128)} %bitcast.12, s32[27,4,128]{2,1,0:T(4,128)} %bitcast.11, f32[1,512]{1,0:T(1,128)} %bitcast.15, f32[96,128]{1,0:T(8,128)} %bitcast.13, s32[4,512]{1,0:T(4,128)} %bitcast.14, s32[4,4096]{1,0:T(4,128)} %bitcast.9, f32[4,4096]{1,0:T(4,128)} %bitcast.10, f32[81,81]{1,0:T(8,128)} %refs_7_.1, ...), custom_call_target="tpu_custom_call" | custom-call | tf_op jit(solution)/shard_map/two_level/pallas_call | solution.py:529
  71.5 1.4 %copy.13 = f32[1,1,3,4096]{3,1,2,0:T(1,128)} copy(f32[1,1,3,4096]{3,1,2,0:T(1,128)} %bitcast.8) | data formatting | bytes 98304

commit v7 on v5

--- a/solution.py
+++ b/solution.py
@@ -205,11 +205,11 @@
     partners = ((down_g, d), (up_g, d), (g, down_d), (g, up_d))
 
     def send_faces(k):
-        for f in range(4):
+        for f in (2, 3, 0, 1):
             for c in range(3):
                 send[k, f, c] = wf[c * FROWS + 4 * f : c * FROWS + 4 * f + 4, :]
         copies = []
-        for f in range(4):
+        for f in (2, 3, 0, 1):
             copy = pltpu.make_async_remote_copy(
                 src_ref=send.at[k, f],
                 dst_ref=recv.at[k, f ^ 1],
@@ -222,15 +222,15 @@
             copies.append(copy)
         return copies
 
-    def add_faces(k, copies):
+    def add_faces(k, faces, copies):
         for copy in copies:
             copy.wait()
-        for f in range(4):
+        for f in faces:
             for c in range(3):
                 at = slice(c * FROWS + 4 * f, c * FROWS + 4 * f + 4)
                 wf[at, :] = wf[at, :] + recv[k, f, c]
 
-    def gather(table, first, rows, fresh, unroll):
+    def gather(table, stride, base, first, rows, fresh, unroll):
         def body(v, carry):
             row = pl.multiple_of(8 * (v // 4), 8)
             lane = pl.multiple_of(128 * (v % 4), 128)
@@ -240,7 +240,8 @@
             else:
                 start = [gath[pl.ds(row + 32 * c, 8), pl.ds(lane, 128)] for c in range(3)]
             got = pick(
-                lambda c, r: table[c * rows + r : c * rows + r + 1, :], rows, hi - first, lo, start
+                lambda c, r: table[c * stride + base + r : c * stride + base + r + 1, :],
+                rows, hi - first, lo, start,
             )
             for c in range(3):
                 gath[pl.ds(row + 32 * c, 8), pl.ds(lane, 128)] = got[c]
@@ -249,10 +250,25 @@
         lax.fori_loop(0, 16, body, 0, unroll=unroll)
 
     def gather_interior():
-        gather(zi, FROWS, ROWS, True, 8)
-
-    def gather_faces():
-        gather(zf, 0, FROWS, False, 8)
+        gather(zi, ROWS, 0, FROWS, ROWS, True, 8)
+
+    def gather_faces(base):
+        gather(zf, FROWS, base, base, 8, False, 8)
+
+    def face_rows(base):
+        return [slice(c * FROWS + base, c * FROWS + base + 8) for c in range(3)]
+
+    def step_faces(k, base):
+        @pl.when(k == 0)
+        def _():
+            for at in face_rows(base):
+                df[at, :] = DAMPING / wf[at, :]
+                zf[at, :] = rf[at, :] * df[at, :]
+
+        @pl.when((k != 0) & (k != 2))
+        def _():
+            for at in face_rows(base):
+                zf[at, :] = zf[at, :] + (rf[at, :] - wf[at, :]) * df[at, :]
 
     home = 6 * (n_dev * g + d)
 
@@ -391,6 +407,7 @@
                 at = slice(c * FROWS + 8 * half, c * FROWS + 8 * half + 8)
                 zf[at, :] = zf[at, :] + got[c]
         gather_interior()
+        gather_faces(0)
 
     def apply(k, carry):
         @pl.when(k == 0)
@@ -441,25 +458,24 @@
         def _():
             gather_interior()
 
-        add_faces(k, copies)
-
-        @pl.when(k == 0)
-        def _():
-            df[...] = DAMPING / wf[...]
-            zf[...] = rf[...] * df[...]
+        add_faces(k, (0, 1), copies[2:])
+        step_faces(k, 0)
+
+        @pl.when((k != 2) & (k != 4))
+        def _():
+            gather_faces(0)
+
+        add_faces(k, (2, 3), copies[:2])
+        step_faces(k, 8)
 
         @pl.when(k == 2)
         def _():
             wf[...] = rf[...] - wf[...]
             coarse_correction()
 
-        @pl.when((k != 0) & (k != 2))
-        def _():
-            zf[...] = zf[...] + (rf[...] - wf[...]) * df[...]
-
         @pl.when(k != 4)
         def _():
-            gather_faces()
+            gather_faces(8)
 
         return carry
 

time: 71 us -> 70.6 us (level)
  no operation moved by 1% of the time
where the time goes in v7:
time: 70.6 us; the launch traced here: 70.5 us
  Pallas kernels  69.1 us (98%)
  local copies, waits for them, and re-layouts  1.42 us (2%)
    pallas_call x1, Pallas kernels, local(): pl.pallas_call(body, name='two_level', out_shape=jax.ShapeDtypeStruct((96...  69.1 us
    unnamed x1, local copies, waits for them, and re-layouts  1.42 us

profile of v7, /device:TPU:1, one launch (start us, length us, event | category | flops | bytes accessed | tf_op | source)
XLA Modules:
  0.0 70.5 jit_solution(6235600251645549617)
XLA Ops:
  0.0 69.1 %two_level.1 = f32[96,128]{1,0:T(8,128)} custom-call(f32[96,128]{1,0:T(8,128)} %bitcast.12, s32[27,4,128]{2,1,0:T(4,128)} %bitcast.11, f32[1,512]{1,0:T(1,128)} %bitcast.15, f32[96,128]{1,0:T(8,128)} %bitcast.13, s32[4,512]{1,0:T(4,128)} %bitcast.14, s32[4,4096]{1,0:T(4,128)} %bitcast.9, f32[4,4096]{1,0:T(4,128)} %bitcast.10, f32[81,81]{1,0:T(8,128)} %refs_7_.1, ...), custom_call_target="tpu_custom_call" | custom-call | tf_op jit(solution)/shard_map/two_level/pallas_call | solution.py:505
  69.1 1.4 %copy.13 = f32[1,1,3,4096]{3,1,2,0:T(1,128)} copy(f32[1,1,3,4096]{3,1,2,0:T(1,128)} %bitcast.8) | data formatting | bytes 98304
